TPU v7x, 32 devices: a whole 2x2x4 slice. The times are simulated.
32 devices in a mesh: vtx: 8 (over y, x, core), edg: 4 (over z).
Axes of the slice: x: 2, y: 2, z: 4, core: 2. Of those that a mesh axis runs over, the one named last changes fastest.
Arguments:
- sketch_cols: bfloat16 [131072, 128], P(('vtx', 'edg')), may hold values from -6 to 6
- edge_weight: float32 [131072], P(('vtx', 'edg')), may hold values from 0.25 to 4
- ground: float32 [16384], P('vtx'), may hold values from 0.05 to 0.5
- src_local: int32 [131072], P(('vtx', 'edg')), may hold values from 0 to 2047
- dst_index: int32 [131072], P(('vtx', 'edg')), may hold values from 0 to 2431
- send_rows: int32 [32, 8, 48], P(('vtx', 'edg')), may hold values from 0 to 2047
- edge_count: int32 [32], P(('vtx', 'edg')), may hold values from 512 to 4096, as said below
Outputs:
- solution: float32 [16384, 128], P('vtx')
- resistance: float32 [131072], P(('vtx', 'edg'))
Inputs may be any that keep to these rules, and one draw needn't show every extreme that they name: `edge_count`: edge slots of a device at positions of its count or beyond are unused. In every draw some device has all 4096 slots live.
All inputs are finite; a program needn't handle non-finite values.
Results may differ from a plain program's by a relative error of at most 0.0003.
Values sent between devices are 32-bit elements; how exact they have to be, the bound alone decides.
A program may use at most 64 MiB of HBM per device.

v0:
```python
import jax
import jax.numpy as jnp
from jax import lax
from jax.sharding import PartitionSpec as P

ITERS = 3


lam_low = 0.05
lam_high = 2.0


def chebyshev_terms(steps):
    centre = (lam_high + lam_low) / 2.0
    half_width = (lam_high - lam_low) / 2.0
    sigma_val = centre / half_width
    rho_prev = 1.0 / sigma_val
    pairs = []
    for count_idx in range(steps - 1):
        rho_next = 1.0 / (2.0 * sigma_val - rho_prev)
        pairs.append((rho_next * rho_prev, 2.0 * rho_next / half_width))
        rho_prev = rho_next
    return (1.0 / centre, pairs)


def fetch(field_in, list_table):
    listed = field_in[list_table]
    arrived = lax.all_to_all(listed, "vtx", split_axis=0, concat_axis=0, tiled=True)
    return jnp.concatenate([field_in, arrived.reshape(-1, field_in.shape[1])], axis=0)


def edge_part(field_in, list_table, flat_rows, sources, targets, weights):
    num_rows = field_in.shape[0]
    extended = fetch(field_in, list_table)
    edge_diffs = weights[:, None] * (field_in[sources] - extended[targets])
    summed = jnp.zeros(extended.shape, jnp.float32)
    summed = summed.at[sources].add(edge_diffs).at[targets].add(-edge_diffs)
    outgoing = summed[num_rows:].reshape(list_table.shape + (field_in.shape[1],))
    returned = lax.all_to_all(outgoing, "vtx", split_axis=0, concat_axis=0, tiled=True)
    return summed[:num_rows].at[flat_rows].add(returned.reshape(-1, field_in.shape[1]))


def local(sketch_cols, edge_weight, ground, src_local, dst_index, send_rows, edge_count):
    blocks = lax.axis_size("vtx")
    num_rows = ground.shape[0]
    num_edges = edge_weight.shape[0]
    slot_width = send_rows.shape[2]
    columns = sketch_cols.shape[1]
    halo_len = blocks * slot_width
    row_lists = send_rows[0]
    flat_list = row_lists.reshape(-1)
    own_table = row_lists[:, None, :]
    live_mask = (jnp.arange(num_edges, dtype=jnp.int32) < edge_count[0]).astype(jnp.float32)
    weight_live = edge_weight * live_mask
    root_live = jnp.sqrt(edge_weight) * live_mask
    edge_terms = root_live[:, None] * sketch_cols.astype(jnp.float32)
    summed = jnp.zeros((num_rows + halo_len, columns), jnp.float32)
    summed = summed.at[src_local].add(edge_terms).at[dst_index].add(-edge_terms)
    degrees = jnp.zeros((num_rows + halo_len,), jnp.float32)
    degrees = degrees.at[src_local].add(weight_live).at[dst_index].add(weight_live)
    back_terms, back_degree = (
        lax.all_to_all(
            summed[num_rows:].reshape(blocks, slot_width, columns),
            "vtx",
            split_axis=0,
            concat_axis=0,
            tiled=True,
        ),
        lax.all_to_all(
            degrees[num_rows:].reshape(blocks, slot_width),
            "vtx",
            split_axis=0,
            concat_axis=0,
            tiled=True,
        ),
    )
    local_side = summed[:num_rows].at[flat_list].add(back_terms.reshape(halo_len, columns))
    local_degree = degrees[:num_rows].at[flat_list].add(back_degree.reshape(halo_len))
    first, pairs = chebyshev_terms(ITERS)
    right_side, degree = lax.psum((local_side, local_degree), "edg")
    inverse = (1.0 / (degree + ground))[:, None]
    residual_now = right_side
    direction = first * inverse * right_side
    solution = jnp.zeros_like(right_side)
    for step_idx in range(ITERS):
        solution = solution + direction
        if step_idx + 1 < ITERS:
            flows = lax.psum(
                edge_part(direction, own_table, flat_list, src_local, dst_index, weight_live), "edg"
            )
            residual_now = residual_now - (ground[:, None] * direction + flows)
            keep_coef, push_coef = pairs[step_idx]
            direction = keep_coef * direction + push_coef * inverse * residual_now
    extended = fetch(solution, own_table)
    gaps = solution[src_local] - extended[dst_index]
    resistance = live_mask * jnp.sum(gaps * gaps, axis=1) / columns
    return (solution, resistance)


def solution(mesh):
    in_specs = (
        P(("vtx", "edg"), None),
        P(("vtx", "edg")),
        P("vtx"),
        P(("vtx", "edg")),
        P(("vtx", "edg")),
        P(("vtx", "edg"), None, None),
        P(("vtx", "edg")),
    )
    out_specs = (P("vtx", None), P(("vtx", "edg")))
    return jax.shard_map(local, mesh=mesh, in_specs=in_specs, out_specs=out_specs, check_vma=False)
```

profile of v0, /device:TPU:0, one launch (start us, length us, event | category | flops | bytes accessed | tf_op | source)
XLA Modules:
  0.0 496.0 jit_solution(15797055523502438406)
XLA Ops:
  10.1 25.0 %scatter_custom_fusion.3 = f32[2432,128]{1,0:T(8,128)S(1)} fusion(s32[4096]{0:T(1024)S(1)} %get-tuple-element.8, bf16[4096,128]{1,0:T(8,128)(2,1)} %param.7, f32[4096]{0:T(1024)S(1)} %get-tuple-element.10, f32[]{:T(128)} %constant.12.clone.1), kind=kCustom, calls=%fused_computation.31 | custom fusion | flops 1572864 | bytes 2310148 | tf_op jit(solution)/shard_map/scatter-add | solution.py:58
  35.2 24.8 %scatter_custom_fusion.4 = f32[2432,128]{1,0:T(8,128)S(1)} fusion(f32[2432,128]{1,0:T(8,128)S(1)} %scatter_custom_fusion.3, s32[4096]{0:T(1024)S(1)} %get-tuple-element.6, bf16[4096,128]{1,0:T(8,128)(2,1)S(1)} %copy-done.7, f32[4096]{0:T(1024)S(1)} %get-tuple-element.10), kind=kCustom, calls=%fused_computation.28 | custom fusion | flops 2097152 | bytes 2310144 | tf_op jit(solution)/shard_map/scatter-add | solution.py:58
  60.7 5.2 %all-to-all-start.1 = ((f32[8,48,128]{2,1,0:T(8,128)}), f32[8,48,128]{2,1,0:T(8,128)S(1)}, u32[]{:S(2)}, u32[]{:S(2)}) async-start(f32[8,48,128]{2,1,0:T(8,128)} %bitcast.1), calls=%async_computation.1 | async-start | bytes 393216 | tf_op jit(solution)/shard_map/all_to_all | solution.py:62
  66.2 6.0 %all-to-all-done.1 = f32[8,48,128]{2,1,0:T(8,128)S(1)} async-done(((f32[8,48,128]{2,1,0:T(8,128)}), f32[8,48,128]{2,1,0:T(8,128)S(1)}, u32[]{:S(2)}, u32[]{:S(2)}) %all-to-all-start.1) | async-done | bytes 196640 | tf_op jit(solution)/shard_map/all_to_all | solution.py:62
  76.1 22.0 %scatter_custom_fusion = f32[2432]{0:T(1024)S(1)} fusion(s32[4096]{0:T(1024)S(1)} %get-tuple-element.8, f32[4096]{0:T(1024)S(1)} %get-tuple-element.9, f32[]{:T(128)} %constant.12.clone.1), kind=kCustom, calls=%fused_computation.58 | custom fusion | flops 4096 | bytes 9732 | tf_op jit(solution)/shard_map/scatter-add | solution.py:60
  98.2 22.4 %scatter_fusion = f32[2432]{0:T(1024)S(1)} fusion(f32[2432]{0:T(1024)S(1)} %scatter_custom_fusion, s32[4096]{0:T(1024)S(1)} %get-tuple-element.6, f32[4096]{0:T(1024)S(1)} %get-tuple-element.9), kind=kCustom, calls=%fused_computation.10 | custom fusion | flops 4096 | bytes 65536 | tf_op jit(solution)/shard_map/scatter-add | solution.py:60
  124.7 4.5 all-to-all-done
  133.6 12.3 %psum.28 = f32[2048]{0:T(1024)S(1)} all-reduce(f32[2048]{0:T(1024)S(1)} %scatter_fusion.1), channel_id=1, replica_groups=mesh['vtx'=8,'edg'=4] {'edg'}, use_global_device_ids=true, to_apply=%region_3.0 | all-reduce | flops 2048 | bytes 16384 | tf_op jit(solution)/shard_map/psum | solution.py:80
  153.3 14.1 %gather_fusion = f32[4096,128]{1,0:T(8,128)} fusion(f32[2048,128]{1,0:T(8,128)S(1)} %broadcast_multiply_fusion, s32[4096]{0:T(1024)S(1)} %get-tuple-element.7), kind=kCustom, calls=%fused_computation | custom fusion | bytes 4210688 | tf_op jit(solution)/shard_map/gather | solution.py:35
  167.5 14.1 %gather_fusion.2 = f32[4096,128]{1,0:T(8,128)} fusion(f32[2432,128]{1,0:T(8,128)S(1)} %pad_maximum_fusion, s32[4096]{0:T(1024)S(1)} %get-tuple-element.5), kind=kCustom, calls=%fused_computation.2 | custom fusion | bytes 4210688 | tf_op jit(solution)/shard_map/gather | solution.py:35
  181.6 25.3 %scatter_custom_fusion.6 = f32[2432,128]{1,0:T(8,128)S(1)} fusion(s32[4096]{0:T(1024)S(1)} %get-tuple-element.8, f32[]{:T(128)} %constant.12.clone.1, f32[4096,128]{1,0:T(8,128)} %gather_fusion, f32[4096,128]{1,0:T(8,128)} %gather_fusion.2, f32[4096]{0:T(1024)S(1)} %get-tuple-element.9), kind=kCustom, calls=%fused_computation.42 | custom fusion | flops 1572864 | bytes 5455876 | tf_op jit(solution)/shard_map/scatter-add | solution.py:37
  206.9 23.1 %scatter_custom_fusion.7 = f32[2432,128]{1,0:T(8,128)S(1)} fusion(f32[2432,128]{1,0:T(8,128)S(1)} %scatter_custom_fusion.6, s32[4096]{0:T(1024)S(1)} %get-tuple-element.6, f32[4096,128]{1,0:T(8,128)S(1)} %copy-done.2, f32[4096,128]{1,0:T(8,128)} %gather_fusion.2, f32[4096]{0:T(1024)S(1)} %get-tuple-element.9), kind=kCustom, calls=%fused_computation.25 | custom fusion | flops 2097152 | bytes 5455872 | tf_op jit(solution)/shard_map/scatter-add | solution.py:37
  230.7 3.9 all-to-all-start.3
  234.7 6.1 %all-to-all-done.3 = f32[8,1,48,128]{3,2,1,0:T(8,128)S(1)} async-done(((f32[8,1,48,128]{3,2,1,0:T(8,128)}), f32[8,1,48,128]{3,2,1,0:T(8,128)S(1)}, u32[]{:S(2)}, u32[]{:S(2)}) %all-to-all-start.3) | async-done | bytes 196640 | tf_op jit(solution)/shard_map/all_to_all | solution.py:39
  244.8 48.4 %all-reduce.6.cloned.1.call-done = f32[2048,128]{1,0:T(8,128)} async-done(((f32[2048,128]{1,0:T(8,128)}), f32[2048,128]{1,0:T(8,128)}) %all-reduce.6.cloned.1.call-update) | async-done | bytes 1048592 | tf_op jit(solution)/shard_map/psum | solution.py:88
  300.5 14.1 %gather_fusion.3 = f32[4096,128]{1,0:T(8,128)} fusion(f32[2048,128]{1,0:T(8,128)S(1)} %multiply_add_fusion, s32[4096]{0:T(1024)S(1)} %copy-done.12), kind=kCustom, calls=%fused_computation.3 | custom fusion | bytes 4210688 | tf_op jit(solution)/shard_map/gather | solution.py:35
  314.7 15.4 %gather_fusion.5 = f32[4096,128]{1,0:T(8,128)} fusion(f32[2432,128]{1,0:T(8,128)S(1)} %pad_maximum_fusion.1, s32[4096]{0:T(1024)} %copy-done.9), kind=kCustom, calls=%fused_computation.5 | custom fusion | bytes 4210688 | tf_op jit(solution)/shard_map/gather | solution.py:35
  330.1 26.0 %scatter_custom_fusion.9 = f32[2432,128]{1,0:T(8,128)} fusion(s32[4096]{0:T(1024)} %copy-done.26, f32[]{:T(128)} %constant.12.clone.1, f32[4096,128]{1,0:T(8,128)} %gather_fusion.3, f32[4096,128]{1,0:T(8,128)} %gather_fusion.5, f32[4096]{0:T(1024)S(1)} %get-tuple-element.9), kind=kCustom, calls=%fused_computation.40 | custom fusion | flops 1572864 | bytes 5456384 | tf_op jit(solution)/shard_map/scatter-add | solution.py:37
  356.2 27.0 %scatter_custom_fusion.10 = f32[2432,128]{1,0:T(8,128)} fusion(f32[2432,128]{1,0:T(8,128)} %scatter_custom_fusion.9, s32[4096]{0:T(1024)} %copy-done.20, f32[4096,128]{1,0:T(8,128)S(1)} %copy-done.1, f32[4096,128]{1,0:T(8,128)} %gather_fusion.5, f32[4096]{0:T(1024)S(1)} %get-tuple-element.9), kind=kCustom, calls=%fused_computation.22 | custom fusion | flops 2097152 | bytes 5455872 | tf_op jit(solution)/shard_map/scatter-add | solution.py:37
  384.8 4.2 all-to-all-start.5
  390.4 4.9 all-to-all-done.5
  399.3 49.5 %all-reduce.8.cloned.1.call-done = f32[2048,128]{1,0:T(8,128)} async-done(((f32[2048,128]{1,0:T(8,128)}), f32[2048,128]{1,0:T(8,128)}) %all-reduce.8.cloned.1.call-update) | async-done | bytes 1048592 | tf_op jit(solution)/shard_map/psum | solution.py:88
  457.2 14.1 %gather_fusion.6 = f32[4096,128]{1,0:T(8,128)} fusion(f32[2048,128]{1,0:T(8,128)S(1)} %add_add_fusion, s32[4096]{0:T(1024)S(1)} %copy-done.13), kind=kCustom, calls=%fused_computation.6 | custom fusion | bytes 4210688 | tf_op jit(solution)/shard_map/gather | solution.py:95
  472.0 14.1 %gather_fusion.8 = f32[4096,128]{1,0:T(8,128)} fusion(f32[2432,128]{1,0:T(8,128)S(1)} %pad_maximum_fusion.2, s32[4096]{0:T(1024)S(1)} %copy-done.10), kind=kCustom, calls=%fused_computation.8 | custom fusion | bytes 4210688 | tf_op jit(solution)/shard_map/gather | solution.py:95
  (106 shorter events, 54.7 us)
Async XLA Ops:
  8.6 144.7 %copy-start.11 = (s32[4096]{0:T(1024)}, s32[4096]{0:T(1024)S(1)}, u32[]{:S(2)}) copy-start(s32[4096]{0:T(1024)S(1)} %get-tuple-element.7) | copy-start | bytes 49156
  8.6 172.9 %copy-start.26 = (s32[4096]{0:T(1024)}, s32[4096]{0:T(1024)S(1)}, u32[]{:S(2)}) copy-start(s32[4096]{0:T(1024)S(1)} %get-tuple-element.8) | copy-start | bytes 49156
  9.4 158.1 %copy-start.9 = (s32[4096]{0:T(1024)}, s32[4096]{0:T(1024)S(1)}, u32[]{:S(2)}) copy-start(s32[4096]{0:T(1024)S(1)} %get-tuple-element.5) | copy-start | bytes 49156
  9.4 197.5 %copy-start.20 = (s32[4096]{0:T(1024)}, s32[4096]{0:T(1024)S(1)}, u32[]{:S(2)}) copy-start(s32[4096]{0:T(1024)S(1)} %get-tuple-element.6) | copy-start | bytes 49156
  60.7 11.4 %all-to-all-start.1 = ((f32[8,48,128]{2,1,0:T(8,128)}), f32[8,48,128]{2,1,0:T(8,128)S(1)}, u32[]{:S(2)}, u32[]{:S(2)}) async-start(f32[8,48,128]{2,1,0:T(8,128)} %bitcast.1), calls=%async_computation.1 | async-start | bytes 393216 | tf_op jit(solution)/shard_map/all_to_all | solution.py:62
  65.9 80.6 %all-reduce.4.cloned.1.call-start = ((), (), s32[]{:S(2)}) async-start(), calls=%async_computation.7 | async-start | bytes 2097152 | tf_op jit(solution)/shard_map/psum | solution.py:80
  66.2 174.6 %copy-start.23 = (s32[384]{0:T(512)}, s32[384]{0:T(512)S(1)}, u32[]{:S(2)}) copy-start(s32[384]{0:T(512)S(1)} %fusion.18) | copy-start | bytes 4612
  121.3 7.9 %all-to-all-start = ((f32[8,1,48]{2,1,0:T(1,128)}), f32[8,1,48]{2,1,0:T(1,128)S(1)}, u32[]{:S(2)}, u32[]{:S(2)}) async-start(f32[8,1,48]{2,1,0:T(1,128)} %all_to_all.24), calls=%async_computation | async-start | bytes 8192 | tf_op jit(solution)/shard_map/all_to_all | solution.py:69
  124.6 170.6 %copy-start.21 = (s32[1024]{0:T(1024)}, s32[1024]{0:T(1024)S(1)}, u32[]{:S(2)}) copy-start(s32[1024]{0:T(1024)S(1)} %pad_clamp_fusion) | copy-start | bytes 12292
  146.5 146.7 %copy-start.14 = (f32[2048]{0:T(1024)}, f32[2048]{0:T(1024)S(1)}, u32[]{:S(2)}) copy-start(f32[2048]{0:T(1024)S(1)} %get-tuple-element.4) | copy-start | bytes 24580
  146.5 146.7 %copy-start.18 = (f32[2048]{0:T(1024)}, f32[2048]{0:T(1024)S(1)}, u32[]{:S(2)}) copy-start(f32[2048]{0:T(1024)S(1)} %get-tuple-element.3) | copy-start | bytes 24580
  149.7 17.7 %all-to-all-start.2 = ((f32[8,1,48,128]{3,2,1,0:T(8,128)}), f32[8,1,48,128]{3,2,1,0:T(8,128)S(1)}, u32[]{:S(2)}, u32[]{:S(2)}) async-start(f32[8,1,48,128]{3,2,1,0:T(8,128)} %bitcast.5), calls=%async_computation.2 | async-start | bytes 393216 | tf_op jit(solution)/shard_map/all_to_all | solution.py:28
  230.7 10.1 %all-to-all-start.3 = ((f32[8,1,48,128]{3,2,1,0:T(8,128)}), f32[8,1,48,128]{3,2,1,0:T(8,128)S(1)}, u32[]{:S(2)}, u32[]{:S(2)}) async-start(f32[8,1,48,128]{3,2,1,0:T(8,128)} %bitcast.8), calls=%async_computation.3 | async-start | bytes 393216 | tf_op jit(solution)/shard_map/all_to_all | solution.py:39
  234.6 58.6 %all-reduce.6.cloned.1.call-start = ((), (), s32[]{:S(2)}) async-start(), calls=%async_computation.8 | async-start | bytes 2097152 | tf_op jit(solution)/shard_map/psum | solution.py:88
  240.8 52.4 %copy-start.6 = (f32[2048,128]{1,0:T(8,128)S(1)}, f32[2048,128]{1,0:T(8,128)}, u32[]{:S(2)}) copy-start(f32[2048,128]{1,0:T(8,128)} %all-reduce.4.cloned.1.call-done) | copy-start | bytes 3145732
  296.9 17.8 %all-to-all-start.4 = ((f32[8,1,48,128]{3,2,1,0:T(8,128)}), f32[8,1,48,128]{3,2,1,0:T(8,128)S(1)}, u32[]{:S(2)}, u32[]{:S(2)}) async-start(f32[8,1,48,128]{3,2,1,0:T(8,128)} %bitcast.11), calls=%async_computation.4 | async-start | bytes 393216 | tf_op jit(solution)/shard_map/all_to_all | solution.py:28
  384.8 10.4 %all-to-all-start.5 = ((f32[8,1,48,128]{3,2,1,0:T(8,128)}), f32[8,1,48,128]{3,2,1,0:T(8,128)S(1)}, u32[]{:S(2)}, u32[]{:S(2)}) async-start(f32[8,1,48,128]{3,2,1,0:T(8,128)} %bitcast.14), calls=%async_computation.5 | async-start | bytes 393216 | tf_op jit(solution)/shard_map/all_to_all | solution.py:39
  389.0 59.7 %all-reduce.8.cloned.1.call-start = ((), (), s32[]{:S(2)}) async-start(), calls=%async_computation.9 | async-start | bytes 2097152 | tf_op jit(solution)/shard_map/psum | solution.py:88
  395.2 53.5 %copy-start.8 = (f32[2048,128]{1,0:T(8,128)S(1)}, f32[2048,128]{1,0:T(8,128)}, u32[]{:S(2)}) copy-start(f32[2048,128]{1,0:T(8,128)} %all-reduce.6.cloned.1.call-done) | copy-start | bytes 3145732
  395.2 53.5 %copy-start.15 = (f32[2048]{0:T(1024)S(1)}, f32[2048]{0:T(1024)}, u32[]{:S(2)}) copy-start(f32[2048]{0:T(1024)} %copy-done.14) | copy-start | bytes 24580
  395.2 53.5 %copy-start.17 = (f32[2048]{0:T(1024)S(1)}, f32[2048]{0:T(1024)}, u32[]{:S(2)}) copy-start(f32[2048]{0:T(1024)} %param.9) | copy-start | bytes 24580
  395.2 53.5 %copy-start.19 = (f32[2048]{0:T(1024)S(1)}, f32[2048]{0:T(1024)}, u32[]{:S(2)}) copy-start(f32[2048]{0:T(1024)} %copy-done.18) | copy-start | bytes 24580
  395.2 53.5 %copy-start.25 = (f32[2048]{0:T(1024)S(1)}, f32[2048]{0:T(1024)}, u32[]{:S(2)}) copy-start(f32[2048]{0:T(1024)} %get-tuple-element.2) | copy-start | bytes 24580
  453.5 17.8 %all-to-all-start.6 = ((f32[8,1,48,128]{3,2,1,0:T(8,128)}), f32[8,1,48,128]{3,2,1,0:T(8,128)S(1)}, u32[]{:S(2)}, u32[]{:S(2)}) async-start(f32[8,1,48,128]{3,2,1,0:T(8,128)} %bitcast.17), calls=%async_computation.6 | async-start | bytes 393216 | tf_op jit(solution)/shard_map/all_to_all | solution.py:28
  (14 other events, 176.6 us)
Sparse Core Ops, SparseCore 0:
  76.3 51.2 all-reduce.3
  244.9 48.2 all-reduce.5
  399.4 49.3 all-reduce.7
where the time goes:
time: 498 us; the launch traced here: 496 us
  other arithmetic  222 us (45%)
  waiting for transfers between devices  119 us (24%)
  local copies, waits for them, and re-layouts  100 us (20%)
  starting transfers between devices  27.6 us (6%)
  between operations  14.9 us (3%)
  blocking collectives  12.3 us (2%)
    scatter-add x4, other arithmetic, edge_part(): summed = summed.at[sources].add(edge_diffs).at[targets].add(-edge_diffs)  101 us
    psum x2, waiting for transfers between devices, local(): lax.psum(edge_part(direction, own_table, flat_list, src_local, dst_index,...  97.9 us
    gather x4, local copies, waits for them, and re-layouts, edge_part(): edge_diffs = weights[:, None] * (field_in[sources] - extended[targets])  57.7 us
    scatter-add x2, other arithmetic, local(): summed = summed.at[src_local].add(edge_terms).at[dst_index].add(-edge_terms)  49.9 us
    scatter-add x2, other arithmetic, local(): degrees.at[src_local].add(weight_live).at[dst_index].add(weight_live)  44.4 us
    gather x2, local copies, waits for them, and re-layouts, local(): gaps = solution[src_local] - extended[dst_index]  28.2 us
    psum x1, blocking collectives, local(): right_side, degree = lax.psum((local_side, local_degree), 'edg')  12.3 us
    all_to_all x2, waiting for transfers between devices, edge_part(): lax.all_to_all(outgoing, 'vtx', split_axis=0, concat_axis=0, tiled=True)  10.9 us
  transfers between devices with their start and end apart: 10, of which 6 were waited for; matrix products, arithmetic and copies ran while one was open for 19% of the time, Pallas kernels for 0%

commit v1 on v0

v1 whole, which is shorter than its diff:
```python
import functools

import jax
import jax.numpy as jnp
from jax import lax
from jax.experimental import pallas as pl
from jax.experimental.pallas import tpu as pltpu
from jax.sharding import PartitionSpec as P

ITERS = 3

lam_low = 0.05
lam_high = 2.0
LANES = 128
VMEM_LIMIT = 60 * 1024 * 1024


def chebyshev_terms(steps):
    centre = (lam_high + lam_low) / 2.0
    half_width = (lam_high - lam_low) / 2.0
    sigma_val = centre / half_width
    rho_prev = 1.0 / sigma_val
    pairs = []
    for count_idx in range(steps - 1):
        rho_next = 1.0 / (2.0 * sigma_val - rho_prev)
        pairs.append((rho_next * rho_prev, 2.0 * rho_next / half_width))
        rho_prev = rho_next
    return (1.0 / centre, pairs)


def split2(x):
    hi = x.astype(jnp.bfloat16)
    lo = (x - hi.astype(jnp.float32)).astype(jnp.bfloat16)
    return hi, lo


def split3(x):
    hi = x.astype(jnp.bfloat16)
    rest = x - hi.astype(jnp.float32)
    mid, lo = split2(rest)
    return hi, mid, lo


def signed(src, dst, shape, axis):
    at = lax.broadcasted_iota(jnp.int32, shape, axis)
    value = jnp.where(at == src, 1.0, jnp.where(at == dst, -1.0, 0.0))
    return value.astype(jnp.bfloat16)


def halves(x):
    n = x.shape[1] // 2
    return x[:, :n] + x[:, n:]


def dot(a, b):
    return jnp.dot(a, b, preferred_element_type=jnp.float32)


def load_field(f_ref, h_ref, field):
    rows = f_ref.shape[0]
    field[:rows, :] = jnp.concatenate(split2(f_ref[...]), axis=1)
    field[rows:, :] = jnp.concatenate(split2(h_ref[...]), axis=1)


def scatter(idxr_ref, values, acc):
    tile = values.shape[0]
    hi_lo = jnp.concatenate(split2(values), axis=1)
    dt = signed(idxr_ref[0:1, :], idxr_ref[1:2, :], (acc.shape[0], tile), 0)
    acc[...] += dot(dt, hi_lo)


def start_kernel(sk_ref, colf_ref, coli_ref, idxr_ref, w_ref, y_ref, deg_ref, acc, dacc):
    step = pl.program_id(0)

    @pl.when(step == 0)
    def _():
        acc[...] = jnp.zeros_like(acc)
        dacc[...] = jnp.zeros_like(dacc)

    terms = colf_ref[:, 0:1] * sk_ref[...].astype(jnp.float32)
    scatter(idxr_ref, terms, acc)
    tile = terms.shape[0]
    high = deg_ref.shape[0]
    weights = w_ref[0:1, :]
    up = lax.broadcasted_iota(jnp.int32, (high, tile), 0)
    lane = lax.broadcasted_iota(jnp.int32, (tile, LANES), 1)
    for k in (0, 1):
        row = idxr_ref[2 + k : 3 + k, :]
        picked = jnp.where(up == row // LANES, weights, 0.0)
        low = jnp.where(lane == coli_ref[:, 2 + k : 3 + k] % LANES, 1.0, 0.0).astype(jnp.bfloat16)
        dacc[...] += dot(jnp.concatenate(split3(picked), axis=0), low)

    @pl.when(step == pl.num_programs(0) - 1)
    def _():
        y_ref[...] = halves(acc[...])
        deg_ref[...] = dacc[:high, :] + dacc[high : 2 * high, :] + dacc[2 * high :, :]


def apply_kernel(f_ref, h_ref, colf_ref, coli_ref, idxr_ref, y_ref, field, acc):
    step = pl.program_id(0)

    @pl.when(step == 0)
    def _():
        acc[...] = jnp.zeros_like(acc)
        load_field(f_ref, h_ref, field)

    tile = coli_ref.shape[0]
    d = signed(coli_ref[:, 0:1], coli_ref[:, 1:2], (tile, field.shape[0]), 1)
    flow = halves(dot(d, field[...])) * colf_ref[:, 1:2]
    scatter(idxr_ref, flow, acc)

    @pl.when(step == pl.num_programs(0) - 1)
    def _():
        y_ref[...] = halves(acc[...])


def gap_kernel(f_ref, h_ref, coli_ref, r_ref, field):
    @pl.when(pl.program_id(0) == 0)
    def _():
        load_field(f_ref, h_ref, field)

    tile = coli_ref.shape[0]
    d = signed(coli_ref[:, 0:1], coli_ref[:, 1:2], (tile, field.shape[0]), 1)
    gap = halves(dot(d, field[...]))
    r_ref[...] = jnp.sum(gap * gap, axis=1, keepdims=True)


def whole(x):
    return pl.BlockSpec(x.shape, lambda i: (0,) * x.ndim)


def tiles(x, tile, axis):
    if axis == 0:
        return pl.BlockSpec((tile, x.shape[1]), lambda i: (i, 0))
    return pl.BlockSpec((x.shape[0], tile), lambda i: (0, i))


def params():
    return pltpu.CompilerParams(dimension_semantics=("arbitrary",), vmem_limit_bytes=VMEM_LIMIT)


def local(sketch_cols, edge_weight, ground, src_local, dst_index, send_rows, edge_count):
    blocks = lax.axis_size("vtx")
    num_rows = ground.shape[0]
    num_edges = edge_weight.shape[0]
    slot_width = send_rows.shape[2]
    columns = sketch_cols.shape[1]
    halo_len = blocks * slot_width
    ext = num_rows + halo_len
    tile = min(512, num_edges)
    grid = (num_edges // tile,)
    row_lists = send_rows[0]
    flat_list = row_lists.reshape(-1)
    live_mask = (jnp.arange(num_edges, dtype=jnp.int32) < edge_count[0]).astype(jnp.float32)
    weight_live = edge_weight * live_mask
    root_live = jnp.sqrt(edge_weight) * live_mask
    loop = src_local == dst_index
    src_d = jnp.where(loop, -1, src_local)
    dst_d = jnp.where(loop, -1, dst_index)
    idx = jnp.stack([src_d, dst_d, src_local, dst_index])
    coli = idx.T
    colf = jnp.stack([root_live, weight_live], axis=1)
    w_row = weight_live[None, :]
    high = -(-(ext // LANES) // 16) * 16

    summed, deg = pl.pallas_call(
        start_kernel,
        grid=grid,
        in_specs=[tiles(sketch_cols, tile, 0), tiles(colf, tile, 0), tiles(coli, tile, 0), tiles(idx, tile, 1), tiles(w_row, tile, 1)],
        out_specs=[pl.BlockSpec((ext, columns), lambda i: (0, 0)), pl.BlockSpec((high, LANES), lambda i: (0, 0))],
        out_shape=[jax.ShapeDtypeStruct((ext, columns), jnp.float32), jax.ShapeDtypeStruct((high, LANES), jnp.float32)],
        scratch_shapes=[pltpu.VMEM((ext, 2 * columns), jnp.float32), pltpu.VMEM((3 * high, LANES), jnp.float32)],
        compiler_params=params(),
        name="start",
    )(sketch_cols, colf, coli, idx, w_row)
    degrees = deg.reshape(-1)[:ext]

    def apply_op(field, arrived):
        return pl.pallas_call(
            apply_kernel,
            grid=grid,
            in_specs=[whole(field), whole(arrived), tiles(colf, tile, 0), tiles(coli, tile, 0), tiles(idx, tile, 1)],
            out_specs=pl.BlockSpec((ext, columns), lambda i: (0, 0)),
            out_shape=jax.ShapeDtypeStruct((ext, columns), jnp.float32),
            scratch_shapes=[pltpu.VMEM((ext, 2 * columns), jnp.bfloat16), pltpu.VMEM((ext, 2 * columns), jnp.float32)],
            compiler_params=params(),
            name="apply",
        )(field, arrived, colf, coli, idx)

    def exchange(x):
        return lax.all_to_all(x, "vtx", split_axis=0, concat_axis=0, tiled=True)

    def give_back(total):
        back = exchange(total[num_rows:].reshape(blocks, slot_width, columns))
        return total[:num_rows].at[flat_list].add(back.reshape(halo_len, columns))

    def fetch(field):
        return exchange(field[row_lists]).reshape(halo_len, columns)

    back_degree = exchange(degrees[num_rows:].reshape(blocks, slot_width))
    local_degree = degrees[:num_rows].at[flat_list].add(back_degree.reshape(halo_len))
    first, pairs = chebyshev_terms(ITERS)
    right_side, degree = lax.psum((give_back(summed), local_degree), "edg")
    inverse = (1.0 / (degree + ground))[:, None]
    residual_now = right_side
    direction = first * inverse * right_side
    solution = jnp.zeros_like(right_side)
    for step_idx in range(ITERS):
        solution = solution + direction
        if step_idx + 1 < ITERS:
            flows = lax.psum(give_back(apply_op(direction, fetch(direction))), "edg")
            residual_now = residual_now - (ground[:, None] * direction + flows)
            keep_coef, push_coef = pairs[step_idx]
            direction = keep_coef * direction + push_coef * inverse * residual_now
    arrived = fetch(solution)
    gaps = pl.pallas_call(
        gap_kernel,
        grid=grid,
        in_specs=[whole(solution), whole(arrived), tiles(coli, tile, 0)],
        out_specs=pl.BlockSpec((tile, 1), lambda i: (i, 0)),
        out_shape=jax.ShapeDtypeStruct((num_edges, 1), jnp.float32),
        scratch_shapes=[pltpu.VMEM((ext, 2 * columns), jnp.bfloat16)],
        compiler_params=params(),
        name="gaps",
    )(solution, arrived, coli)
    resistance = live_mask * gaps[:, 0] / columns
    return (solution, resistance)


def solution(mesh):
    in_specs = (
        P(("vtx", "edg"), None),
        P(("vtx", "edg")),
        P("vtx"),
        P(("vtx", "edg")),
        P(("vtx", "edg")),
        P(("vtx", "edg"), None, None),
        P(("vtx", "edg")),
    )
    out_specs = (P("vtx", None), P(("vtx", "edg")))
    return jax.shard_map(local, mesh=mesh, in_specs=in_specs, out_specs=out_specs, check_vma=False)
```

time: 498 us -> 342 us (0.69)
  other arithmetic: 222 us -> 23.5 us
  local copies, waits for them, and re-layouts: 100 us -> 18.1 us
  Pallas kernels: 0 us -> 81.1 us
  blocking collectives: 12.3 us -> 42.1 us
  waiting for transfers between devices: 119 us -> 146 us
  starting transfers between devices: 27.6 us -> 15.4 us
    scatter-add x11 -> x3, other arithmetic: 205 us -> 9.18 us  [give_back(): return total[:num_rows].at[flat_list].add(back.reshape(halo_len, columns))]
    gather x9 -> x3, local copies, waits for them, and re-layouts: 90.7 us -> 3.37 us  [fetch(): return exchange(field[row_lists]).reshape(halo_len, columns)]
    pallas_call x0 -> x4, Pallas kernels: none -> 81.1 us  [the longest x2 53.8 us: apply_op(): pl.pallas_call(apply_kernel, grid=grid, in_specs=[whole(field), whole(arr...]
    all_to_all x0 -> x3, blocking collectives: none -> 29.3 us  [exchange(): return lax.all_to_all(x, 'vtx', split_axis=0, concat_axis=0, tiled=True)]
    psum x3, waiting for transfers between devices: 97.9 us -> 125 us  [the longest x2 99 us: local(): flows = lax.psum(give_back(apply_op(direction, fetch(direction))), 'edg')]
    all_to_all x7 -> x4, starting transfers between devices: 27.5 us -> 15.3 us  [exchange(): return lax.all_to_all(x, 'vtx', split_axis=0, concat_axis=0, tiled=True)]
    all_to_all x7 -> x4, waiting for transfers between devices: 21.4 us -> 21.4 us  [exchange(): return lax.all_to_all(x, 'vtx', split_axis=0, concat_axis=0, tiled=True)]
  transfers between devices with their start and end apart: 10 -> 7, of which waited for: 6 -> 7; matrix products, arithmetic and copies ran while one was open for 19% -> 2% of each run, Pallas kernels for 0% -> 0%
where the time goes in v1:
time: 342 us; the launch traced here: 341 us
  waiting for transfers between devices  146 us (43%)
  Pallas kernels  81.1 us (24%)
  blocking collectives  42.1 us (12%)
  other arithmetic  23.5 us (7%)
  local copies, waits for them, and re-layouts  18.1 us (5%)
  starting transfers between devices  15.4 us (5%)
  between operations  14.7 us (4%)
    psum x2, waiting for transfers between devices, local(): flows = lax.psum(give_back(apply_op(direction, fetch(direction))), 'edg')  99 us
    pallas_call x2, Pallas kernels, apply_op(): pl.pallas_call(apply_kernel, grid=grid, in_specs=[whole(field), whole(arr...  53.8 us
    all_to_all x3, blocking collectives, exchange(): return lax.all_to_all(x, 'vtx', split_axis=0, concat_axis=0, tiled=True)  29.3 us
    psum x1, waiting for transfers between devices, local(): right_side, degree = lax.psum((give_back(summed), local_degree), 'edg')  25.9 us
    all_to_all x4, waiting for transfers between devices, exchange(): return lax.all_to_all(x, 'vtx', split_axis=0, concat_axis=0, tiled=True)  21.4 us
    all_to_all x4, starting transfers between devices, exchange(): return lax.all_to_all(x, 'vtx', split_axis=0, concat_axis=0, tiled=True)  15.3 us
    pallas_call x1, Pallas kernels, local(): pl.pallas_call(start_kernel, grid=grid, in_specs=[tiles(sketch_cols, tile...  14.6 us
    psum x1, blocking collectives, local(): right_side, degree = lax.psum((give_back(summed), local_degree), 'edg')  12.8 us
  transfers between devices with their start and end apart: 7, of which 7 were waited for; matrix products, arithmetic and copies ran while one was open for 2% of the time, Pallas kernels for 0%

profile of v1, /device:TPU:0, one launch (start us, length us, event | category | flops | bytes accessed | tf_op | source)
XLA Modules:
  0.0 341.2 jit_solution(11558997139780296824)
XLA Ops:
  12.7 14.6 %start.1 = (f32[2432,128]{1,0:T(8,128)}, f32[32,128]{1,0:T(8,128)}) custom-call(bf16[4096,128]{1,0:T(8,128)(2,1)} %sk_ref.1, f32[4096,2]{1,0:T(8,128)} %copy.22.colf_ref, s32[4096,4]{1,0:T(8,128)} %bitcast.30, s32[4,4096]{1,0:T(4,128)} %copy-done.8, f32[1,4096]{1,0:T(1,128)} %bitcast.44), custom_call_target="tpu_custom_call" | custom-call | tf_op jit(solution)/shard_map/start/pallas_call | solution.py:166
  28.9 5.2 %all-to-all-start.1 = ((f32[8,48,128]{2,1,0:T(8,128)}), f32[8,48,128]{2,1,0:T(8,128)S(1)}, u32[]{:S(2)}, u32[]{:S(2)}) async-start(f32[8,48,128]{2,1,0:T(8,128)} %bitcast.11), calls=%async_computation.1 | async-start | bytes 393216 | tf_op jit(solution)/shard_map/all_to_all | solution.py:191
  35.6 4.7 %all-to-all-done.1 = f32[8,48,128]{2,1,0:T(8,128)S(1)} async-done(((f32[8,48,128]{2,1,0:T(8,128)}), f32[8,48,128]{2,1,0:T(8,128)S(1)}, u32[]{:S(2)}, u32[]{:S(2)}) %all-to-all-start.1) | async-done | bytes 196640 | tf_op jit(solution)/shard_map/all_to_all | solution.py:191
  40.3 3.0 scatter_fusion.1
  45.0 3.3 all-to-all-start
  48.4 4.4 %all-to-all-done = f32[8,1,48]{2,1,0:T(1,128)S(1)} async-done(((f32[8,1,48]{2,1,0:T(1,128)}), f32[8,1,48]{2,1,0:T(1,128)S(1)}, u32[]{:S(2)}, u32[]{:S(2)}) %all-to-all-start) | async-done | bytes 1568 | tf_op jit(solution)/shard_map/all_to_all | solution.py:191
  54.1 3.3 scatter_fusion
  57.5 12.8 %psum.28 = f32[2048]{0:T(1024)S(1)} all-reduce(f32[2048]{0:T(1024)S(1)} %scatter_fusion), channel_id=1, replica_groups=mesh['vtx'=8,'edg'=4] {'edg'}, use_global_device_ids=true, to_apply=%region_1.2 | all-reduce | flops 2048 | bytes 16384 | tf_op jit(solution)/shard_map/psum | solution.py:203
  70.3 25.9 %all-reduce.4.cloned.1.call-done = f32[2048,128]{1,0:T(8,128)} async-done(((f32[2048,128]{1,0:T(8,128)}), f32[2048,128]{1,0:T(8,128)}) %all-reduce.4.cloned.1.call-update) | async-done | bytes 1048592 | tf_op jit(solution)/shard_map/psum | solution.py:203
  98.9 9.8 %all_to_all.39 = f32[8,48,128]{2,1,0:T(8,128)} all-to-all(f32[8,48,128]{2,1,0:T(8,128)S(1)} %bitcast.40), channel_id=1, replica_groups=mesh['vtx'=8,'edg'=4] {'vtx'}, dimensions={0} | all-to-all | bytes 393216 | tf_op jit(solution)/shard_map/all_to_all | solution.py:191
  108.7 26.9 %apply.2 = f32[2432,128]{1,0:T(8,128)} custom-call(f32[2048,128]{1,0:T(8,128)} %copy-done.1, f32[384,128]{1,0:T(8,128)} %bitcast.35, f32[4096,2]{1,0:T(8,128)} %copy.22.colf_ref, s32[4096,4]{1,0:T(8,128)} %bitcast.31, s32[4,4096]{1,0:T(4,128)} %copy-done.8), custom_call_target="tpu_custom_call" | custom-call | tf_op jit(solution)/shard_map/apply/pallas_call | solution.py:179
  137.3 3.4 all-to-all-start.3
  140.7 6.1 %all-to-all-done.3 = f32[8,48,128]{2,1,0:T(8,128)S(1)} async-done(((f32[8,48,128]{2,1,0:T(8,128)}), f32[8,48,128]{2,1,0:T(8,128)S(1)}, u32[]{:S(2)}, u32[]{:S(2)}) %all-to-all-start.3) | async-done | bytes 196640 | tf_op jit(solution)/shard_map/all_to_all | solution.py:191
  146.8 3.2 scatter_fusion.2
  151.0 49.5 %all-reduce.6.cloned.1.call-done = f32[2048,128]{1,0:T(8,128)} async-done(((f32[2048,128]{1,0:T(8,128)}), f32[2048,128]{1,0:T(8,128)}) %all-reduce.6.cloned.1.call-update) | async-done | bytes 1048592 | tf_op jit(solution)/shard_map/psum | solution.py:211
  203.7 9.8 %all_to_all.40 = f32[8,48,128]{2,1,0:T(8,128)} all-to-all(f32[8,48,128]{2,1,0:T(8,128)S(1)} %bitcast.41), channel_id=1, replica_groups=mesh['vtx'=8,'edg'=4] {'vtx'}, dimensions={0} | all-to-all | bytes 393216 | tf_op jit(solution)/shard_map/all_to_all | solution.py:191
  213.5 26.9 %apply.3 = f32[2432,128]{1,0:T(8,128)} custom-call(f32[2048,128]{1,0:T(8,128)} %copy-done, f32[384,128]{1,0:T(8,128)} %bitcast.34, f32[4096,2]{1,0:T(8,128)} %copy.22.colf_ref, s32[4096,4]{1,0:T(8,128)} %bitcast.32, s32[4,4096]{1,0:T(4,128)} %copy-done.8), custom_call_target="tpu_custom_call" | custom-call | tf_op jit(solution)/shard_map/apply/pallas_call | solution.py:179
  242.0 3.4 all-to-all-start.5
  245.5 6.1 %all-to-all-done.5 = f32[8,48,128]{2,1,0:T(8,128)S(1)} async-done(((f32[8,48,128]{2,1,0:T(8,128)}), f32[8,48,128]{2,1,0:T(8,128)S(1)}, u32[]{:S(2)}, u32[]{:S(2)}) %all-to-all-start.5) | async-done | bytes 196640 | tf_op jit(solution)/shard_map/all_to_all | solution.py:191
  251.6 3.0 scatter_fusion.3
  255.6 49.5 %all-reduce.8.cloned.1.call-done = f32[2048,128]{1,0:T(8,128)} async-done(((f32[2048,128]{1,0:T(8,128)}), f32[2048,128]{1,0:T(8,128)}) %all-reduce.8.cloned.1.call-update) | async-done | bytes 1048592 | tf_op jit(solution)/shard_map/psum | solution.py:211
  305.1 3.1 add_add_fusion.f_ref
  309.3 9.8 %all_to_all.41 = f32[8,48,128]{2,1,0:T(8,128)} all-to-all(f32[8,48,128]{2,1,0:T(8,128)S(1)} %bitcast.39), channel_id=1, replica_groups=mesh['vtx'=8,'edg'=4] {'vtx'}, dimensions={0} | all-to-all | bytes 393216 | tf_op jit(solution)/shard_map/all_to_all | solution.py:191
  319.1 12.8 %gaps.1 = f32[4096,1]{1,0:T(8,128)} custom-call(f32[2048,128]{1,0:T(8,128)} %copy-done.5, f32[384,128]{1,0:T(8,128)} %bitcast.42, s32[4096,4]{1,0:T(8,128)} %bitcast.33), custom_call_target="tpu_custom_call" | custom-call | tf_op jit(solution)/shard_map/gaps/pallas_call | solution.py:216
  (69 shorter events, 26.1 us)
Async XLA Ops:
  7.2 3.4 %copy-start.11 = (s32[4096]{0:T(1024)S(1)}, s32[4096]{0:T(1024)}, u32[]{:S(2)}) copy-start(s32[4096]{0:T(1024)} %param.11) | copy-start | bytes 49156
  7.2 3.4 %copy-start.12 = (s32[4096]{0:T(1024)S(1)}, s32[4096]{0:T(1024)}, u32[]{:S(2)}) copy-start(s32[4096]{0:T(1024)} %param.10) | copy-start | bytes 49156
  8.6 4.1 %copy-start.9 = (f32[4096]{0:T(1024)}, f32[4096]{0:T(1024)S(1)}, u32[]{:S(2)}) copy-start(f32[4096]{0:T(1024)S(1)} %get-tuple-element.12) | copy-start | bytes 49156
  10.7 2.0 copy-start.8
  27.3 8.2 %copy-start.13 = (s32[1,8,48]{2,1,0:T(8,128)S(1)}, s32[1,8,48]{2,1,0:T(8,128)}, u32[]{:S(2)}) copy-start(s32[1,8,48]{2,1,0:T(8,128)} %param.12) | copy-start | bytes 4612
  28.9 11.4 %all-to-all-start.1 = ((f32[8,48,128]{2,1,0:T(8,128)}), f32[8,48,128]{2,1,0:T(8,128)S(1)}, u32[]{:S(2)}, u32[]{:S(2)}) async-start(f32[8,48,128]{2,1,0:T(8,128)} %bitcast.11), calls=%async_computation.1 | async-start | bytes 393216 | tf_op jit(solution)/shard_map/all_to_all | solution.py:191
  34.1 62.1 %all-reduce.4.cloned.1.call-start = ((), (), s32[]{:S(2)}) async-start(), calls=%async_computation.7 | async-start | bytes 2097152 | tf_op jit(solution)/shard_map/psum | solution.py:203
  40.3 4.0 %copy-start.14 = (f32[32,128]{1,0:T(8,128)S(1)}, f32[32,128]{1,0:T(8,128)}, u32[]{:S(2)}) copy-start(f32[32,128]{1,0:T(8,128)} %get-tuple-element.4) | copy-start | bytes 49156
  43.3 1.0 copy-start.2
  45.0 7.9 %all-to-all-start = ((f32[8,1,48]{2,1,0:T(1,128)}), f32[8,1,48]{2,1,0:T(1,128)S(1)}, u32[]{:S(2)}, u32[]{:S(2)}) async-start(f32[8,1,48]{2,1,0:T(1,128)} %bitcast.10), calls=%async_computation | async-start | bytes 8192 | tf_op jit(solution)/shard_map/all_to_all | solution.py:191
  54.1 16.1 %copy-start.10 = (f32[2048]{0:T(1024)S(1)}, f32[2048]{0:T(1024)}, u32[]{:S(2)}) copy-start(f32[2048]{0:T(1024)} %param.9) | copy-start | bytes 24580
  97.8 10.9 %copy-start.1 = (f32[2048,128]{1,0:T(8,128)}, f32[2048,128]{1,0:T(8,128)S(1)}, u32[]{:S(2)}) copy-start(f32[2048,128]{1,0:T(8,128)S(1)} %broadcast_multiply_fusion.f_ref) | copy-start | bytes 3145732
  135.6 11.2 %slice-start.1 = ((f32[2432,128]{1,0:T(8,128)}), f32[2048,128]{1,0:T(8,128)S(1)}, s32[]{:S(2)}) async-start(f32[2432,128]{1,0:T(8,128)} %apply.2), calls=%async_computation.11 | async-start | bytes 2097152 | tf_op jit(solution)/shard_map/slice | solution.py:195
  137.3 9.5 %all-to-all-start.3 = ((f32[8,48,128]{2,1,0:T(8,128)}), f32[8,48,128]{2,1,0:T(8,128)S(1)}, u32[]{:S(2)}, u32[]{:S(2)}) async-start(f32[8,48,128]{2,1,0:T(8,128)} %bitcast.16), calls=%async_computation.3 | async-start | bytes 393216 | tf_op jit(solution)/shard_map/all_to_all | solution.py:191
  140.7 59.8 %all-reduce.6.cloned.1.call-start = ((), (), s32[]{:S(2)}) async-start(), calls=%async_computation.8 | async-start | bytes 2097152 | tf_op jit(solution)/shard_map/psum | solution.py:211
  146.8 53.7 %copy-start.6 = (f32[2048,128]{1,0:T(8,128)S(1)}, f32[2048,128]{1,0:T(8,128)}, u32[]{:S(2)}) copy-start(f32[2048,128]{1,0:T(8,128)} %all-reduce.4.cloned.1.call-done) | copy-start | bytes 3145732
  150.0 1.0 copy-start.4
  202.6 10.9 %copy-start = (f32[2048,128]{1,0:T(8,128)}, f32[2048,128]{1,0:T(8,128)S(1)}, u32[]{:S(2)}) copy-start(f32[2048,128]{1,0:T(8,128)S(1)} %multiply_add_fusion.f_ref) | copy-start | bytes 3145732
  240.3 11.2 %slice-start = ((f32[2432,128]{1,0:T(8,128)}), f32[2048,128]{1,0:T(8,128)S(1)}, s32[]{:S(2)}) async-start(f32[2432,128]{1,0:T(8,128)} %apply.3), calls=%async_computation.10 | async-start | bytes 2097152 | tf_op jit(solution)/shard_map/slice | solution.py:195
  242.0 9.5 %all-to-all-start.5 = ((f32[8,48,128]{2,1,0:T(8,128)}), f32[8,48,128]{2,1,0:T(8,128)S(1)}, u32[]{:S(2)}, u32[]{:S(2)}) async-start(f32[8,48,128]{2,1,0:T(8,128)} %bitcast.20), calls=%async_computation.5 | async-start | bytes 393216 | tf_op jit(solution)/shard_map/all_to_all | solution.py:191
  245.4 59.6 %all-reduce.8.cloned.1.call-start = ((), (), s32[]{:S(2)}) async-start(), calls=%async_computation.9 | async-start | bytes 2097152 | tf_op jit(solution)/shard_map/psum | solution.py:211
  251.6 53.5 %copy-start.7 = (f32[2048,128]{1,0:T(8,128)S(1)}, f32[2048,128]{1,0:T(8,128)}, u32[]{:S(2)}) copy-start(f32[2048,128]{1,0:T(8,128)} %all-reduce.6.cloned.1.call-done) | copy-start | bytes 3145732
  254.6 1.0 copy-start.3
  308.2 10.9 %copy-start.5 = (f32[2048,128]{1,0:T(8,128)}, f32[2048,128]{1,0:T(8,128)S(1)}, u32[]{:S(2)}) copy-start(f32[2048,128]{1,0:T(8,128)S(1)} %add_add_fusion.f_ref) | copy-start | bytes 3145732
Sparse Core Ops, SparseCore 0:
  44.4 51.7 all-reduce.3
  151.1 49.3 all-reduce.5
  255.7 49.3 all-reduce.7

commit v2 on v1

--- a/solution.py
+++ b/solution.py
@@ -123,6 +123,237 @@
     d = signed(coli_ref[:, 0:1], coli_ref[:, 1:2], (tile, field.shape[0]), 1)
     gap = halves(dot(d, field[...]))
     r_ref[...] = jnp.sum(gap * gap, axis=1, keepdims=True)
+
+
+def slot_copy(src, dst, send_sem, recv_sem, target):
+    return pltpu.make_async_remote_copy(
+        src_ref=src, dst_ref=dst, send_sem=send_sem, recv_sem=recv_sem,
+        device_id=target, device_id_type=pl.DeviceIdType.MESH,
+    )
+
+
+def all_to_all(me, peers, src, dst, send_sem, recv_sem):
+    for off in range(1, peers):
+        to = lax.rem(me + off, peers)
+        slot_copy(src(to), dst.at[me], send_sem.at[off], recv_sem.at[off], {"vtx": to}).start()
+
+
+def all_to_all_wait(me, peers, src, dst, send_sem, recv_sem):
+    for off in range(1, peers):
+        to = lax.rem(me + off, peers)
+        origin = lax.rem(me + peers - off, peers)
+        slot_copy(src(to), dst.at[origin], send_sem.at[off], recv_sem.at[off], {"vtx": to}).wait()
+
+
+def line_sum(z, pieces, own, outer, inner, mine, result, send_sem, outer_sem, inner_sem):
+    count = len(pieces)
+
+    def copy(kind, k, src, dst, sem, target):
+        rows = pl.ds(*pieces[k])
+        return slot_copy(src.at[rows], dst.at[rows], send_sem.at[kind, k], sem.at[k], {"edg": target})
+
+    @pl.when((z + 1) // 2 % 2 == 0)
+    def _():
+        near = 1 + z // 3
+        for k in range(count):
+            copy(0, k, own, outer, outer_sem, near).start()
+        for k in range(count):
+            copy(0, k, own, outer, outer_sem, near).wait_recv()
+            rows = pl.ds(*pieces[k])
+            result[rows, :] = outer[rows, :]
+        for k in range(count):
+            copy(0, k, own, outer, outer_sem, near).wait_send()
+
+    def middle(side):
+        far, peer = 3 * side, 2 - side
+        lag_total, lag_pass = 2, 4
+        for t in range(count + lag_pass):
+            if t < count:
+                rows = pl.ds(*pieces[t])
+                copy(1, t, own, outer, outer_sem, far).wait_recv()
+                if t % 2 != side:
+                    mine[rows, :] = own[rows, :] + outer[rows, :]
+                    copy(0, t, mine, inner, inner_sem, peer).start()
+            k = t - lag_total
+            if 0 <= k < count and k % 2 == side:
+                rows = pl.ds(*pieces[k])
+                copy(0, k, mine, inner, inner_sem, peer).wait_recv()
+                total = (own[rows, :] + outer[rows, :]) + inner[rows, :]
+                mine[rows, :] = total
+                copy(0, k, mine, inner, inner_sem, peer).start()
+                copy(1, k, mine, outer, outer_sem, far).start()
+                result[rows, :] = total
+            k = t - lag_pass
+            if 0 <= k < count and k % 2 != side:
+                rows = pl.ds(*pieces[k])
+                copy(0, k, mine, inner, inner_sem, peer).wait_recv()
+                copy(1, k, inner, outer, outer_sem, far).start()
+                result[rows, :] = inner[rows, :]
+        for k in range(count):
+            copy(0, k, mine, inner, inner_sem, peer).wait_send()
+            copy(1, k, mine if k % 2 == side else inner, outer, outer_sem, far).wait_send()
+
+    for side in (0, 1):
+        pl.when(z == 1 + side)(functools.partial(middle, side))
+
+
+def stage_kernel(stage, peers, pieces, *refs):
+    first, pairs = chebyshev_terms(ITERS)
+    last = stage == ITERS - 1
+    refs = list(refs)
+
+    def take(n):
+        got = refs[:n]
+        del refs[:n]
+        return got
+
+    y_ref, rows_smem, list_ref, ground_ref = take(4)
+    if stage == 0:
+        deg_ref, degh_ref, padrow_ref, padcol_ref = take(4)
+    else:
+        res_in, dir_in, inv_in = take(3)
+        sol_in = take(1)[0] if stage > 1 else dir_in
+    if stage == 0:
+        dir_ref, res_ref, inv_ref, arr_ref = take(4)
+        listed_from = dir_ref
+    elif not last:
+        dir_ref, res_ref, sol_ref, arr_ref = take(4)
+        listed_from = dir_ref
+    else:
+        sol_ref, arr_ref = take(2)
+        listed_from = sol_ref
+    own, outer, inner, mine, result, back, listed, landed = take(8)
+    back_send, back_recv, land_send, land_recv, line_send, outer_sem, inner_sem = take(7)
+    if stage == 0:
+        dback, dback_send, dback_recv = take(3)
+
+    me, z = lax.axis_index("vtx"), lax.axis_index("edg")
+    slot = back.shape[1]
+    num_rows = ground_ref.shape[0]
+    columns = y_ref.shape[1]
+    middle = (z + 1) // 2 % 2
+
+    barrier = pltpu.get_barrier_semaphore()
+
+    def greet(target):
+        pl.semaphore_signal(barrier, inc=1, device_id=target, device_id_type=pl.DeviceIdType.MESH)
+
+    for off in range(1, peers):
+        greet({"vtx": lax.rem(me + off, peers)})
+
+    @pl.when(z > 0)
+    def _():
+        greet({"edg": z - 1})
+
+    @pl.when(z < 3)
+    def _():
+        greet({"edg": z + 1})
+
+    pl.semaphore_wait(barrier, peers + middle)
+
+    def halo_of(to):
+        return y_ref.at[pl.ds(pl.multiple_of(num_rows + to * slot, 8), slot)]
+
+    def degree_of(to):
+        return degh_ref.at[to]
+
+    all_to_all(me, peers, halo_of, back, back_send, back_recv)
+    if stage == 0:
+        all_to_all(me, peers, degree_of, dback, dback_send, dback_recv)
+    back[me] = y_ref[pl.ds(pl.multiple_of(num_rows + me * slot, 8), slot), :]
+    if stage == 0:
+        dback[me] = degh_ref[me]
+    all_to_all_wait(me, peers, halo_of, back, back_send, back_recv)
+    returned = jnp.concatenate(split2(back[...].reshape(peers * slot, columns)), axis=1)
+    step = 256 if num_rows % 256 == 0 else num_rows
+    for at in range(0, num_rows, step):
+        row = lax.broadcasted_iota(jnp.int32, (step, peers * slot), 0) + at
+        pick = jnp.where(row == list_ref[...], 1.0, 0.0).astype(jnp.bfloat16)
+        own[at : at + step, :] = y_ref[at : at + step, :] + halves(dot(pick, returned))
+    if stage == 0:
+        all_to_all_wait(me, peers, degree_of, dback, dback_send, dback_recv)
+        high = num_rows // LANES
+        values = jnp.concatenate([dback[q, 0:1, :] for q in range(peers)], axis=1)
+        up = lax.broadcasted_iota(jnp.int32, (high, values.shape[1]), 0)
+        picked = jnp.where(up == padrow_ref[...] // LANES, values, 0.0)
+        lane = lax.broadcasted_iota(jnp.int32, (values.shape[1], LANES), 1)
+        low = jnp.where(lane == padcol_ref[...] % LANES, 1.0, 0.0).astype(jnp.bfloat16)
+        parts = dot(jnp.concatenate(split3(picked), axis=0), low)
+        own[num_rows:, :] = deg_ref[:high, :] + (parts[:high] + parts[high : 2 * high] + parts[2 * high :])
+
+    line_sum(z, pieces, own, outer, inner, mine, result, line_send, outer_sem, inner_sem)
+
+    eye = lax.broadcasted_iota(jnp.int32, (LANES, LANES), 0) == lax.broadcasted_iota(jnp.int32, (LANES, LANES), 1)
+    for at in range(0, num_rows, LANES):
+        rows = slice(at, at + LANES)
+        if stage == 0:
+            row = at // LANES
+            degree = result[num_rows + row : num_rows + row + 1, :]
+            column = jnp.sum(jnp.where(eye, degree, 0.0), axis=1, keepdims=True)
+            inverse = 1.0 / (column + ground_ref[rows, :])
+            inv_ref[rows, :] = inverse
+            res_ref[rows, :] = result[rows, :]
+            dir_ref[rows, :] = first * inverse * result[rows, :]
+        else:
+            keep_coef, push_coef = pairs[stage - 1]
+            residual = res_in[rows, :] - (ground_ref[rows, :] * dir_in[rows, :] + result[rows, :])
+            direction = keep_coef * dir_in[rows, :] + push_coef * inv_in[rows, :] * residual
+            if not last:
+                res_ref[rows, :] = residual
+                dir_ref[rows, :] = direction
+            sol_ref[rows, :] = sol_in[rows, :] + direction
+
+    def pick_rows(h, _):
+        for q in range(peers):
+            listed[q, pl.ds(h, 1), :] = listed_from[pl.ds(rows_smem[q, h], 1), :]
+        return 0
+
+    lax.fori_loop(0, slot, pick_rows, 0)
+
+    def listed_of(to):
+        return listed.at[to]
+
+    all_to_all(me, peers, listed_of, landed, land_send, land_recv)
+    landed[me] = listed[me]
+    all_to_all_wait(me, peers, listed_of, landed, land_send, land_recv)
+    arr_ref[...] = landed[...].reshape(peers * slot, columns)
+
+
+def run_stage(stage, peers, slot, num_rows, columns, operands):
+    extra = num_rows // LANES if stage == 0 else 0
+    size = 128
+    pieces = [(num_rows, extra)] if extra else []
+    pieces += [(at, size) for at in range(0, num_rows, size)]
+    count = len(pieces)
+    total = num_rows + extra
+    f32 = jnp.float32
+    field = jax.ShapeDtypeStruct((num_rows, columns), f32)
+    arrived = jax.ShapeDtypeStruct((peers * slot, columns), f32)
+    if stage == 0:
+        outs = [field, field, jax.ShapeDtypeStruct((num_rows, 1), f32), arrived]
+    elif stage < ITERS - 1:
+        outs = [field, field, field, arrived]
+    else:
+        outs = [field, arrived]
+    vmem = pl.BlockSpec(memory_space=pltpu.VMEM)
+    in_specs = [vmem] * len(operands)
+    in_specs[1] = pl.BlockSpec(memory_space=pltpu.SMEM)
+    dma = pltpu.SemaphoreType.DMA
+    buffer = pltpu.VMEM((total, columns), f32)
+    halo = pltpu.VMEM((peers, slot, columns), f32)
+    scratch = [buffer] * 5 + [halo] * 3
+    scratch += [dma((peers,))] * 4 + [dma((2, count)), dma((count,)), dma((count,))]
+    if stage == 0:
+        scratch += [pltpu.VMEM((peers, 8, LANES), f32), dma((peers,)), dma((peers,))]
+    return pl.pallas_call(
+        functools.partial(stage_kernel, stage, peers, pieces),
+        in_specs=in_specs,
+        out_specs=[vmem] * len(outs),
+        out_shape=outs,
+        scratch_shapes=scratch,
+        compiler_params=pltpu.CompilerParams(collective_id=stage, has_side_effects=True, vmem_limit_bytes=VMEM_LIMIT),
+        name="stage%d" % stage,
+    )(*operands)
 
 
 def whole(x):
@@ -173,7 +404,6 @@
         compiler_params=params(),
         name="start",
     )(sketch_cols, colf, coli, idx, w_row)
-    degrees = deg.reshape(-1)[:ext]
 
     def apply_op(field, arrived):
         return pl.pallas_call(
@@ -187,32 +417,24 @@
             name="apply",
         )(field, arrived, colf, coli, idx)
 
-    def exchange(x):
-        return lax.all_to_all(x, "vtx", split_axis=0, concat_axis=0, tiled=True)
-
-    def give_back(total):
-        back = exchange(total[num_rows:].reshape(blocks, slot_width, columns))
-        return total[:num_rows].at[flat_list].add(back.reshape(halo_len, columns))
-
-    def fetch(field):
-        return exchange(field[row_lists]).reshape(halo_len, columns)
-
-    back_degree = exchange(degrees[num_rows:].reshape(blocks, slot_width))
-    local_degree = degrees[:num_rows].at[flat_list].add(back_degree.reshape(halo_len))
-    first, pairs = chebyshev_terms(ITERS)
-    right_side, degree = lax.psum((give_back(summed), local_degree), "edg")
-    inverse = (1.0 / (degree + ground))[:, None]
-    residual_now = right_side
-    direction = first * inverse * right_side
-    solution = jnp.zeros_like(right_side)
-    for step_idx in range(ITERS):
-        solution = solution + direction
-        if step_idx + 1 < ITERS:
-            flows = lax.psum(give_back(apply_op(direction, fetch(direction))), "edg")
-            residual_now = residual_now - (ground[:, None] * direction + flows)
-            keep_coef, push_coef = pairs[step_idx]
-            direction = keep_coef * direction + push_coef * inverse * residual_now
-    arrived = fetch(solution)
+    flat_row = flat_list[None, :]
+    ground_col = ground[:, None]
+    pad_list = jnp.pad(row_lists, ((0, 0), (0, LANES - slot_width)), constant_values=-1).reshape(-1)
+    degrees = jnp.pad(deg.reshape(-1)[num_rows:ext].reshape(blocks, slot_width), ((0, 0), (0, LANES - slot_width)))
+    degree_out = jnp.broadcast_to(degrees[:, None, :], (blocks, 8, LANES))
+    stage = functools.partial(run_stage, peers=blocks, slot=slot_width, num_rows=num_rows, columns=columns)
+    common = (row_lists, flat_row, ground_col)
+    direction, residual, inverse, arrived = stage(
+        0, operands=(summed,) + common + (deg, degree_out, pad_list[None, :], pad_list[:, None])
+    )
+    state = (residual, direction, inverse)
+    for step_idx in range(1, ITERS):
+        summed = apply_op(direction, arrived)
+        if step_idx < ITERS - 1:
+            direction, residual, solution, arrived = stage(step_idx, operands=(summed,) + common + state)
+            state = (residual, direction, inverse, solution)
+        else:
+            solution, arrived = stage(step_idx, operands=(summed,) + common + state)
     gaps = pl.pallas_call(
         gap_kernel,
         grid=grid,

time: 342 us -> 265 us (0.77)
  Pallas kernels: 81.1 us -> 246 us
  waiting for transfers between devices: 146 us -> 0 us
  blocking collectives: 42.1 us -> 0 us
  other arithmetic: 23.5 us -> 5.21 us
  starting transfers between devices: 15.4 us -> 0 us
  between operations: 14.7 us -> 1.35 us
  local copies, waits for them, and re-layouts: 18.1 us -> 11.4 us
    pallas_call x0 -> x3, Pallas kernels: none -> 165 us  [run_stage(): pl.pallas_call(functools.partial(stage_kernel, stage, peers, pieces), in_...]
    psum x3 -> x0, waiting for transfers between devices: 125 us -> none  [the longest x2 99 us: local(): flows = lax.psum(give_back(apply_op(direction, fetch(direction))), 'edg')]
    all_to_all x3 -> x0, blocking collectives: 29.3 us -> none  [exchange(): return lax.all_to_all(x, 'vtx', split_axis=0, concat_axis=0, tiled=True)]
    all_to_all x4 -> x0, waiting for transfers between devices: 21.4 us -> none  [exchange(): return lax.all_to_all(x, 'vtx', split_axis=0, concat_axis=0, tiled=True)]
    all_to_all x4 -> x0, starting transfers between devices: 15.3 us -> none  [exchange(): return lax.all_to_all(x, 'vtx', split_axis=0, concat_axis=0, tiled=True)]
    psum x1 -> x0, blocking collectives: 12.8 us -> none  [local(): right_side, degree = lax.psum((give_back(summed), local_degree), 'edg')]
    scatter-add x4 -> x0, other arithmetic: 12.5 us -> none  [the longest x3 9.18 us: give_back(): return total[:num_rows].at[flat_list].add(back.reshape(halo_len, columns))]
    slice x10 -> x1, local copies, waits for them, and re-layouts: 6.34 us -> 0.68 us  [local(): deg.reshape(-1)[num_rows:ext].reshape(blocks, slot_width)]
  transfers between devices with their start and end apart: 7 -> 0, of which waited for: 7 -> 0; matrix products, arithmetic and copies ran while one was open for 2% -> 0% of each run, Pallas kernels for 0% -> 0%
where the time goes in v2:
time: 265 us; the launch traced here: 264 us
  Pallas kernels  246 us (93%)
  local copies, waits for them, and re-layouts  11.4 us (4%)
  other arithmetic  5.21 us (2%)
    pallas_call x3, Pallas kernels, run_stage(): pl.pallas_call(functools.partial(stage_kernel, stage, peers, pieces), in_...  165 us
    pallas_call x2, Pallas kernels, apply_op(): pl.pallas_call(apply_kernel, grid=grid, in_specs=[whole(field), whole(arr...  53.8 us
    pallas_call x1, Pallas kernels, local(): pl.pallas_call(start_kernel, grid=grid, in_specs=[tiles(sketch_cols, tile...  14.6 us
    pallas_call x1, Pallas kernels, local(): pl.pallas_call(gap_kernel, grid=grid, in_specs=[whole(solution), whole(ar...  12.8 us

profile of v2, /device:TPU:0, one launch (start us, length us, event | category | flops | bytes accessed | tf_op | source)
XLA Modules:
  0.0 264.2 jit_solution(10749074447110689586)
XLA Ops:
  1.3 1.3 broadcast_in_dim_reshape_squeeze.3.refs_2_
  2.6 0.7 pad.9
  3.3 0.7 sqrt_select_fusion
  4.0 0.0 copy-start.2
  4.1 0.7 compare_select_fusion.1
  4.8 0.8 pad_add_fusion.idxr_ref
  5.6 0.0 copy-start.1
  5.6 1.1 copy.29.refs_7_
  6.7 2.0 copy.28.refs_3_
  8.7 2.0 copy.27.colf_ref
  10.7 2.0 copy.26
  12.7 14.6 %start.1 = (f32[2432,128]{1,0:T(8,128)}, f32[32,128]{1,0:T(8,128)}) custom-call(bf16[4096,128]{1,0:T(8,128)(2,1)} %sk_ref.1, f32[4096,2]{1,0:T(8,128)} %copy.27.colf_ref, s32[4096,4]{1,0:T(8,128)} %bitcast.15, s32[4,4096]{1,0:T(4,128)} %copy-done.1, f32[1,4096]{1,0:T(1,128)} %bitcast.20), custom_call_target="tpu_custom_call" | custom-call | tf_op jit(solution)/shard_map/start/pallas_call | solution.py:397
  27.3 0.7 slice.4
  28.0 0.1 reshape.11
  28.1 0.6 broadcast_in_dim.20.refs_5_
  28.7 56.0 %stage0.1 = (f32[2048,128]{1,0:T(8,128)}, f32[2048,128]{1,0:T(8,128)}, f32[2048,1]{1,0:T(8,128)}, f32[384,128]{1,0:T(8,128)}) custom-call(f32[2432,128]{1,0:T(8,128)} %get-tuple-element.14.refs_0_, s32[8,48]{1,0:T(8,128)} %bitcast.22, s32[1,384]{1,0:T(1,128)} %broadcast_in_dim_reshape_squeeze.3.refs_2_, f32[2048,1]{1,0:T(8,128)} %copy.28.refs_3_, ...), custom_call_target="tpu_custom_call" | custom-call | tf_op jit(solution)/shard_map/stage0/pallas_call | solution.py:348
  84.6 26.9 %apply.2.refs_0_ = f32[2432,128]{1,0:T(8,128)} custom-call(f32[2048,128]{1,0:T(8,128)} %get-tuple-element.16.f_ref.refs_5_, f32[384,128]{1,0:T(8,128)} %get-tuple-element.17.h_ref, f32[4096,2]{1,0:T(8,128)} %copy.27.colf_ref, s32[4096,4]{1,0:T(8,128)} %bitcast.16, s32[4,4096]{1,0:T(4,128)} %copy-done.1), custom_call_target="tpu_custom_call" | custom-call | tf_op jit(solution)/shard_map/apply/pallas_call | solution.py:409
  111.5 55.3 %stage1.1 = (f32[2048,128]{1,0:T(8,128)}, f32[2048,128]{1,0:T(8,128)}, f32[2048,128]{1,0:T(8,128)}, f32[384,128]{1,0:T(8,128)}) custom-call(f32[2432,128]{1,0:T(8,128)} %apply.2.refs_0_, s32[8,48]{1,0:T(8,128)} %bitcast.23, s32[1,384]{1,0:T(1,128)} %broadcast_in_dim_reshape_squeeze.3.refs_2_, f32[2048,1]{1,0:T(8,128)} %copy.28.refs_3_, ...), custom_call_target="tpu_custom_call" | custom-call | tf_op jit(solution)/shard_map/stage1/pallas_call | solution.py:348
  166.8 26.9 %apply.3.refs_0_ = f32[2432,128]{1,0:T(8,128)} custom-call(f32[2048,128]{1,0:T(8,128)} %get-tuple-element.20.f_ref.refs_5_, f32[384,128]{1,0:T(8,128)} %get-tuple-element.21.h_ref, f32[4096,2]{1,0:T(8,128)} %copy.27.colf_ref, s32[4096,4]{1,0:T(8,128)} %bitcast.17, s32[4,4096]{1,0:T(4,128)} %copy-done.1), custom_call_target="tpu_custom_call" | custom-call | tf_op jit(solution)/shard_map/apply/pallas_call | solution.py:409
  193.7 53.7 %stage2.1 = (f32[2048,128]{1,0:T(8,128)}, f32[384,128]{1,0:T(8,128)}) custom-call(f32[2432,128]{1,0:T(8,128)} %apply.3.refs_0_, s32[8,48]{1,0:T(8,128)} %bitcast.24, s32[1,384]{1,0:T(1,128)} %broadcast_in_dim_reshape_squeeze.3.refs_2_, f32[2048,1]{1,0:T(8,128)} %copy.28.refs_3_, f32[2048,128]{1,0:T(8,128)} %get-tuple-element.22.refs_4_, ...), custom_call_target="tpu_custom_call" | custom-call | tf_op jit(solution)/shard_map/stage2/pallas_call | solution.py:348
  247.5 12.8 %gaps.1 = f32[4096,1]{1,0:T(8,128)} custom-call(f32[2048,128]{1,0:T(8,128)} %get-tuple-element.32.f_ref, f32[384,128]{1,0:T(8,128)} %get-tuple-element.25.h_ref, s32[4096,4]{1,0:T(8,128)} %bitcast.18), custom_call_target="tpu_custom_call" | custom-call | tf_op jit(solution)/shard_map/gaps/pallas_call | solution.py:438
  260.3 2.3 reduce
  262.6 0.6 select_multiply_fusion
  263.2 1.0 copy.36
  (8 shorter events, 0.1 us)
Async XLA Ops:
  3.3 9.4 %copy-start.3 = (s32[8,128]{1,0:T(8,128)}, s32[8,128]{1,0:T(8,128)S(1)}, u32[]{:S(2)}) copy-start(s32[8,128]{1,0:T(8,128)S(1)} %pad.9) | copy-start | bytes 12292
  4.0 8.7 %copy-start.2 = (f32[4096]{0:T(1024)}, f32[4096]{0:T(1024)S(1)}, u32[]{:S(2)}) copy-start(f32[4096]{0:T(1024)S(1)} %get-tuple-element.29) | copy-start | bytes 49156
  5.6 7.1 %copy-start.1 = (s32[4,4096]{1,0:T(4,128)}, s32[4,4096]{1,0:T(4,128)S(1)}, u32[]{:S(2)}) copy-start(s32[4,4096]{1,0:T(4,128)S(1)} %pad_add_fusion.idxr_ref) | copy-start | bytes 196612
  260.3 2.9 %copy-start = (f32[2048,128]{1,0:T(8,128)S(1)}, f32[2048,128]{1,0:T(8,128)}, u32[]{:S(2)}) copy-start(f32[2048,128]{1,0:T(8,128)} %get-tuple-element.32.f_ref) | copy-start | bytes 3145732

commit v3 on v0

v3 whole, which is shorter than its diff:
```python
import functools

import jax
import jax.numpy as jnp
from jax import lax
from jax.experimental import pallas as pl
from jax.experimental.pallas import tpu as pltpu
from jax.sharding import PartitionSpec as P

ITERS = 3

lam_low = 0.05
lam_high = 2.0
LANES = 128
VMEM_LIMIT = 60 * 1024 * 1024


def chebyshev_terms(steps):
    centre = (lam_high + lam_low) / 2.0
    half_width = (lam_high - lam_low) / 2.0
    sigma_val = centre / half_width
    rho_prev = 1.0 / sigma_val
    pairs = []
    for count_idx in range(steps - 1):
        rho_next = 1.0 / (2.0 * sigma_val - rho_prev)
        pairs.append((rho_next * rho_prev, 2.0 * rho_next / half_width))
        rho_prev = rho_next
    return (1.0 / centre, pairs)


def split2(x):
    hi = x.astype(jnp.bfloat16)
    lo = (x - hi.astype(jnp.float32)).astype(jnp.bfloat16)
    return hi, lo


def split3(x):
    hi = x.astype(jnp.bfloat16)
    rest = x - hi.astype(jnp.float32)
    mid, lo = split2(rest)
    return hi, mid, lo


def signed(src, dst, shape, axis):
    at = lax.broadcasted_iota(jnp.int32, shape, axis)
    value = jnp.where(at == src, 1.0, jnp.where(at == dst, -1.0, 0.0))
    return value.astype(jnp.bfloat16)


def halves(x):
    n = x.shape[1] // 2
    return x[:, :n] + x[:, n:]


def dot(a, b):
    return jnp.dot(a, b, preferred_element_type=jnp.float32)


def even_piece(total, most):
    return max(n for n in range(8, most + 1, 8) if total % n == 0)


def slot_copy(src, dst, send_sem, recv_sem, target):
    return pltpu.make_async_remote_copy(
        src_ref=src, dst_ref=dst, send_sem=send_sem, recv_sem=recv_sem,
        device_id=target, device_id_type=pl.DeviceIdType.MESH,
    )


def all_to_all(me, peers, src, dst, send_sem, recv_sem):
    for off in range(1, peers):
        to = lax.rem(me + off, peers)
        slot_copy(src(to), dst.at[me], send_sem.at[off], recv_sem.at[off], {"vtx": to}).start()


def all_to_all_wait(me, peers, src, dst, send_sem, recv_sem):
    for off in range(1, peers):
        to = lax.rem(me + off, peers)
        origin = lax.rem(me + peers - off, peers)
        slot_copy(src(to), dst.at[origin], send_sem.at[off], recv_sem.at[off], {"vtx": to}).wait()


class LineSum:
    lag_total, lag_pass = 2, 4

    def __init__(self, z, pieces, own, outer, inner, mine, result, send_sem, outer_sem, inner_sem):
        self.z, self.pieces, self.own, self.outer, self.inner = z, pieces, own, outer, inner
        self.mine, self.result, self.send_sem = mine, result, send_sem
        self.outer_sem, self.inner_sem = outer_sem, inner_sem
        self.near = 1 + z // 3

    def copy(self, kind, k, src, dst, sem, target):
        rows = pl.ds(*self.pieces[k])
        return slot_copy(src.at[rows], dst.at[rows], self.send_sem.at[kind, k], sem.at[k], {"edg": target})

    def end_copy(self, k):
        return self.copy(0, k, self.own, self.outer, self.outer_sem, self.near)

    def at_end(self, work):
        pl.when((self.z + 1) // 2 % 2 == 0)(work)

    def at_middle(self, work):
        for side in (0, 1):
            pl.when(self.z == 1 + side)(functools.partial(work, side))

    def send_group(self, ks):
        def work():
            for k in ks:
                self.end_copy(k).start()

        self.at_end(work)

    def step(self, side, t):
        own, outer, inner, mine, result = self.own, self.outer, self.inner, self.mine, self.result
        count = len(self.pieces)
        far, peer = 3 * side, 2 - side
        if t < count:
            rows = pl.ds(*self.pieces[t])
            self.copy(1, t, own, outer, self.outer_sem, far).wait_recv()
            if t % 2 != side:
                mine[rows, :] = own[rows, :] + outer[rows, :]
                self.copy(0, t, mine, inner, self.inner_sem, peer).start()
        k = t - self.lag_total
        if 0 <= k < count and k % 2 == side:
            rows = pl.ds(*self.pieces[k])
            self.copy(0, k, mine, inner, self.inner_sem, peer).wait_recv()
            total = (own[rows, :] + outer[rows, :]) + inner[rows, :]
            mine[rows, :] = total
            self.copy(0, k, mine, inner, self.inner_sem, peer).start()
            self.copy(1, k, mine, outer, self.outer_sem, far).start()
            result[rows, :] = total
        k = t - self.lag_pass
        if 0 <= k < count and k % 2 != side:
            rows = pl.ds(*self.pieces[k])
            self.copy(0, k, mine, inner, self.inner_sem, peer).wait_recv()
            self.copy(1, k, inner, outer, self.outer_sem, far).start()
            result[rows, :] = inner[rows, :]

    def pass_group(self, ts):
        def work(side):
            for t in ts:
                self.step(side, t)

        self.at_middle(work)

    def finish(self):
        count = len(self.pieces)

        def end():
            for k in range(count):
                self.end_copy(k).wait_recv()
                rows = pl.ds(*self.pieces[k])
                self.result[rows, :] = self.outer[rows, :]
            for k in range(count):
                self.end_copy(k).wait_send()

        def middle(side):
            for k in range(count):
                self.copy(0, k, self.mine, self.inner, self.inner_sem, 2 - side).wait_send()
                source = self.mine if k % 2 == side else self.inner
                self.copy(1, k, source, self.outer, self.outer_sem, 3 * side).wait_send()

        self.at_end(end)
        self.at_middle(middle)


def stage_kernel(stage, peers, groups, pieces, *refs):
    first, pairs = chebyshev_terms(ITERS)
    last = stage == ITERS - 1
    refs = list(refs)

    def take(n):
        got = refs[:n]
        del refs[:n]
        return got

    g_ref, rows_smem, idx_ref, flt_ref, list_ref, ground_ref = take(6)
    if stage == 0:
        (list8_ref,) = take(1)
    else:
        res_in, dir_in, inv_in = take(3)
        sol_in = take(1)[0] if stage > 1 else dir_in
    if stage == 0:
        dir_ref, res_ref, inv_ref, gout_ref = take(4)
        listed_from = dir_ref
    elif not last:
        dir_ref, res_ref, sol_ref, gout_ref = take(4)
        listed_from = dir_ref
    else:
        sol_ref, gap_ref = take(2)
        listed_from = sol_ref
    own, outer, inner, mine, result, yhalo, back, listed, landed = take(9)
    idxc, fltc, field, part, retb, acc = take(6)
    back_send, back_recv, land_send, land_recv, line_send, outer_sem, inner_sem = take(7)
    if stage == 0:
        flows, degh, dback, dback_send, dback_recv = take(5)
    else:
        flows = g_ref

    me, z = lax.axis_index("vtx"), lax.axis_index("edg")
    slot, columns = back.shape[1], back.shape[2]
    halo_len = peers * slot
    num_rows = ground_ref.shape[0] * LANES
    num_edges = idx_ref.shape[1]
    etile = min(512, num_edges)
    ktile = min(1024, num_edges)

    barrier = pltpu.get_barrier_semaphore()

    def greet(target):
        pl.semaphore_signal(barrier, inc=1, device_id=target, device_id_type=pl.DeviceIdType.MESH)

    for off in range(1, peers):
        greet({"vtx": lax.rem(me + off, peers)})

    @pl.when(z > 0)
    def _():
        greet({"edg": z - 1})

    @pl.when(z < 3)
    def _():
        greet({"edg": z + 1})

    idxc[...] = idx_ref[...].T
    fltc[...] = flt_ref[...].T

    if stage == 0:

        def make_terms(k, _):
            rows = pl.ds(pl.multiple_of(k * etile, etile), etile)
            terms = fltc[rows, 0:1] * g_ref[rows, :].astype(jnp.float32)
            flows[rows, :] = jnp.concatenate(split2(terms), axis=1)
            return 0

        lax.fori_loop(0, num_edges // etile, make_terms, 0)
        weights = flt_ref[1:2, :]
        lane = lax.broadcasted_iota(jnp.int32, (num_edges, LANES), 1)

        def count_up(high, row, column):
            up = lax.broadcasted_iota(jnp.int32, (high, num_edges), 0)
            picked = jnp.where(up == row, weights, 0.0)
            low = jnp.where(lane == column, 1.0, 0.0).astype(jnp.bfloat16)
            parts = dot(jnp.concatenate(split3(picked), axis=0), low)
            return parts[:high] + parts[high : 2 * high] + parts[2 * high :]

        high = num_rows // LANES
        up_rows = -(-high // 16) * 16
        degree_own = count_up(up_rows, idx_ref[2:3, :] // LANES, idxc[:, 2:3] % LANES)
        degree_own += count_up(up_rows, idx_ref[3:4, :] // LANES, idxc[:, 3:4] % LANES)
        own[num_rows:, :] = degree_own[:high]
        degree_far = count_up(-(-peers // 16) * 16, idx_ref[4:5, :], idxc[:, 5:6])
        for q in range(peers):
            degh[q] = jnp.broadcast_to(degree_far[q : q + 1, :], (8, LANES))

    def scatter_rows(at, rows):
        acc[:rows, :] = jnp.zeros((rows, 2 * columns), jnp.float32)

        def body(k, _):
            cols = pl.ds(pl.multiple_of(k * ktile, ktile), ktile)
            pick = signed(idx_ref[0:1, cols] - at, idx_ref[1:2, cols] - at, (rows, ktile), 0)
            acc[:rows, :] += dot(pick, flows[cols, :])
            return 0

        lax.fori_loop(0, num_edges // ktile, body, 0)
        return halves(acc[:rows, :])

    hpiece = even_piece(halo_len, 512)
    for at in range(0, halo_len, hpiece):
        yhalo[at : at + hpiece, :] = scatter_rows(num_rows + at, hpiece)

    pl.semaphore_wait(barrier, peers + (z + 1) // 2 % 2)

    def halo_of(to):
        return yhalo.at[pl.ds(pl.multiple_of(to * slot, 8), slot)]

    def degree_of(to):
        return degh.at[to]

    all_to_all(me, peers, halo_of, back, back_send, back_recv)
    back[me] = yhalo[pl.ds(pl.multiple_of(me * slot, 8), slot), :]
    if stage == 0:
        all_to_all(me, peers, degree_of, dback, dback_send, dback_recv)
        dback[me] = degh[me]

    line = LineSum(z, pieces, own, outer, inner, mine, result, line_send, outer_sem, inner_sem)
    for c, (at, size, ks) in enumerate(groups):
        local_sum = scatter_rows(at, size)
        if c == 0:
            all_to_all_wait(me, peers, halo_of, back, back_send, back_recv)
            retb[...] = jnp.concatenate(split2(back[...].reshape(halo_len, columns)), axis=1)
            if stage == 0:
                all_to_all_wait(me, peers, degree_of, dback, dback_send, dback_recv)
                cols8 = list8_ref[...].T
                up = lax.broadcasted_iota(jnp.int32, (high, LANES), 0)
                lane = lax.broadcasted_iota(jnp.int32, (LANES, LANES), 1)
                for q in range(peers):
                    picked = jnp.where(up == list8_ref[q : q + 1, :] // LANES, dback[q, 0:1, :], 0.0)
                    low = jnp.where(lane == cols8[:, q : q + 1] % LANES, 1.0, 0.0).astype(jnp.bfloat16)
                    parts = dot(jnp.concatenate(split3(picked), axis=0), low)
                    own[num_rows:, :] += parts[:high] + parts[high : 2 * high] + parts[2 * high :]
        row = lax.broadcasted_iota(jnp.int32, (size, halo_len), 0)
        pick = jnp.where(row == list_ref[...] - at, 1.0, 0.0).astype(jnp.bfloat16)
        own[at : at + size, :] = local_sum + halves(dot(pick, retb[...]))
        line.send_group(ks)
        if c > 0:
            line.pass_group(groups[c - 1][2])
    line.pass_group(list(groups[-1][2]) + list(range(len(pieces), len(pieces) + line.lag_pass)))
    line.finish()

    ground_cols = ground_ref[...].T
    if stage == 0:
        inverse = 1.0 / (result[num_rows:, :] + ground_ref[...])
        inv_ref[...] = inverse
    else:
        inverse = inv_in[...]
    inverse_cols = inverse.T
    for at in range(0, num_rows, LANES):
        rows = slice(at, at + LANES)
        j = at // LANES
        inv_col, ground_col = inverse_cols[:, j : j + 1], ground_cols[:, j : j + 1]
        if stage == 0:
            res_ref[rows, :] = result[rows, :]
            shown = first * inv_col * result[rows, :]
            dir_ref[rows, :] = shown
        else:
            keep_coef, push_coef = pairs[stage - 1]
            residual = res_in[rows, :] - (ground_col * dir_in[rows, :] + result[rows, :])
            direction = keep_coef * dir_in[rows, :] + push_coef * inv_col * residual
            total = sol_in[rows, :] + direction
            sol_ref[rows, :] = total
            shown = total
            if not last:
                res_ref[rows, :] = residual
                dir_ref[rows, :] = direction
                shown = direction
        field[rows, :] = jnp.concatenate(split2(shown), axis=1)

    def pick_rows(h, _):
        for q in range(peers):
            listed[q, pl.ds(h, 1), :] = listed_from[pl.ds(rows_smem[q, h], 1), :]
        return 0

    lax.fori_loop(0, slot, pick_rows, 0)

    def listed_of(to):
        return listed.at[to]

    all_to_all(me, peers, listed_of, landed, land_send, land_recv)
    landed[me] = listed[me]

    def gather_near(k, _):
        rows = pl.ds(pl.multiple_of(k * etile, etile), etile)
        d = signed(idxc[rows, 0:1], idxc[rows, 1:2], (etile, num_rows), 1)
        part[rows, :] = halves(dot(d, field[:num_rows, :]))
        return 0

    lax.fori_loop(0, num_edges // etile, gather_near, 0)
    all_to_all_wait(me, peers, listed_of, landed, land_send, land_recv)
    field[num_rows:, :] = jnp.concatenate(split2(landed[...].reshape(halo_len, columns)), axis=1)

    def gather_far(k):
        rows = pl.ds(k * etile, etile)
        d = signed(idxc[rows, 0:1] - num_rows, idxc[rows, 1:2] - num_rows, (etile, halo_len), 1)
        return rows, part[rows, :] + halves(dot(d, field[num_rows:, :]))

    if not last:

        def make_flows(k, _):
            k = pl.multiple_of(k * etile, etile) // etile
            rows, gap = gather_far(k)
            gout_ref[rows, :] = jnp.concatenate(split2(gap * fltc[rows, 1:2]), axis=1)
            return 0

        lax.fori_loop(0, num_edges // etile, make_flows, 0)
    else:
        lane = lax.broadcasted_iota(jnp.int32, (LANES, LANES), 1)
        wide = num_edges // LANES
        for base in range(0, wide, LANES):
            sums = jnp.zeros((LANES, LANES), jnp.float32)
            for k in range(base * LANES // etile, min(wide, base + LANES) * LANES // etile):
                _, gap = gather_far(k)
                square = jnp.sum(gap * gap, axis=1, keepdims=True)
                for i in range(etile // LANES):
                    j = k * (etile // LANES) + i - base
                    sums = jnp.where(lane == j, square[i * LANES : (i + 1) * LANES, :], sums)
            take_rows = min(LANES, wide - base)
            gap_ref[base : base + take_rows, :] = sums.T[:take_rows, :]


def run_stage(stage, peers, slot, num_rows, columns, num_edges, operands):
    high = num_rows // LANES
    extra = high if stage == 0 else 0
    size, big = 128, 512
    pieces = [(at, size) for at in range(0, num_rows, size)]
    groups = [[at, big, list(range(at // size, (at + big) // size))] for at in range(0, num_rows, big)]
    if extra:
        groups[-1][2].append(len(pieces))
        pieces.append((num_rows, extra))
    count = len(pieces)
    f32, bf16, i32 = jnp.float32, jnp.bfloat16, jnp.int32
    halo_len = peers * slot
    field = jax.ShapeDtypeStruct((num_rows, columns), f32)
    flows = jax.ShapeDtypeStruct((num_edges, 2 * columns), bf16)
    if stage == 0:
        outs = [field, field, jax.ShapeDtypeStruct((high, LANES), f32), flows]
    elif stage < ITERS - 1:
        outs = [field, field, field, flows]
    else:
        outs = [field, jax.ShapeDtypeStruct((num_edges // LANES, LANES), f32)]
    vmem = pl.BlockSpec(memory_space=pltpu.VMEM)
    in_specs = [vmem] * len(operands)
    in_specs[1] = pl.BlockSpec(memory_space=pltpu.SMEM)
    dma = pltpu.SemaphoreType.DMA
    buffer = pltpu.VMEM((num_rows + extra, columns), f32)
    halo = pltpu.VMEM((peers, slot, columns), f32)
    scratch = [buffer] * 5 + [pltpu.VMEM((halo_len, columns), f32)] + [halo] * 3
    scratch += [pltpu.VMEM((num_edges, 8), i32), pltpu.VMEM((num_edges, 8), f32)]
    scratch += [pltpu.VMEM((num_rows + halo_len, 2 * columns), bf16), pltpu.VMEM((num_edges, columns), f32)]
    scratch += [pltpu.VMEM((halo_len, 2 * columns), bf16), pltpu.VMEM((big, 2 * columns), f32)]
    scratch += [dma((peers,))] * 4 + [dma((2, count)), dma((count,)), dma((count,))]
    if stage == 0:
        scratch += [pltpu.VMEM((num_edges, 2 * columns), bf16)]
        scratch += [pltpu.VMEM((peers, 8, LANES), f32)] * 2 + [dma((peers,)), dma((peers,))]
    return pl.pallas_call(
        functools.partial(stage_kernel, stage, peers, groups, pieces),
        in_specs=in_specs,
        out_specs=[vmem] * len(outs),
        out_shape=outs,
        scratch_shapes=scratch,
        compiler_params=pltpu.CompilerParams(collective_id=stage, has_side_effects=True, vmem_limit_bytes=VMEM_LIMIT),
        name="stage%d" % stage,
    )(*operands)


def local(sketch_cols, edge_weight, ground, src_local, dst_index, send_rows, edge_count):
    blocks = lax.axis_size("vtx")
    num_rows = ground.shape[0]
    num_edges = edge_weight.shape[0]
    slot_width = send_rows.shape[2]
    columns = sketch_cols.shape[1]
    row_lists = send_rows[0]
    live_mask = (jnp.arange(num_edges, dtype=jnp.int32) < edge_count[0]).astype(jnp.float32)
    weight_live = edge_weight * live_mask
    root_live = jnp.sqrt(edge_weight) * live_mask
    loop = src_local == dst_index
    slots = dst_index - num_rows
    peer = jnp.where(slots < 0, -1, slots // slot_width)
    within = jnp.where(slots < 0, -1, slots % slot_width)
    idx = jnp.stack(
        [jnp.where(loop, -1, src_local), jnp.where(loop, -1, dst_index), src_local, dst_index, peer, within, loop.astype(jnp.int32), peer]
    )
    zero = jnp.zeros_like(root_live)
    flt = jnp.stack([root_live, weight_live] + [zero] * 6)
    flat_row = row_lists.reshape(1, -1)
    ground_rows = ground.reshape(num_rows // LANES, LANES)
    list8 = jnp.pad(row_lists, ((0, 0), (0, LANES - slot_width)), constant_values=-1)
    stage = functools.partial(
        run_stage, peers=blocks, slot=slot_width, num_rows=num_rows, columns=columns, num_edges=num_edges
    )
    common = (row_lists, idx, flt, flat_row, ground_rows)
    direction, residual, inverse, flows = stage(0, operands=(sketch_cols,) + common + (list8,))
    state = (residual, direction, inverse)
    for step_idx in range(1, ITERS):
        if step_idx < ITERS - 1:
            direction, residual, solution, flows = stage(step_idx, operands=(flows,) + common + state)
            state = (residual, direction, inverse, solution)
        else:
            solution, gaps = stage(step_idx, operands=(flows,) + common + state)
    resistance = live_mask * gaps.reshape(-1) / columns
    return (solution, resistance)


def solution(mesh):
    in_specs = (
        P(("vtx", "edg"), None),
        P(("vtx", "edg")),
        P("vtx"),
        P(("vtx", "edg")),
        P(("vtx", "edg")),
        P(("vtx", "edg"), None, None),
        P(("vtx", "edg")),
    )
    out_specs = (P("vtx", None), P(("vtx", "edg")))
    return jax.shard_map(local, mesh=mesh, in_specs=in_specs, out_specs=out_specs, check_vma=False)
```

time: 498 us -> 215 us (0.43)
  other arithmetic: 222 us -> 4.29 us
  Pallas kernels: 0 us -> 202 us
  waiting for transfers between devices: 119 us -> 0 us
  local copies, waits for them, and re-layouts: 100 us -> 6.57 us
  starting transfers between devices: 27.6 us -> 0 us
  between operations: 14.9 us -> 1.32 us
  blocking collectives: 12.3 us -> 0 us
    scatter-add x12 -> x0, other arithmetic: 208 us -> none  [the longest x4 101 us: edge_part(): summed = summed.at[sources].add(edge_diffs).at[targets].add(-edge_diffs)]
    pallas_call x0 -> x3, Pallas kernels: none -> 202 us  [run_stage(): pl.pallas_call(functools.partial(stage_kernel, stage, peers, groups, piec...]
    psum x3 -> x0, waiting for transfers between devices: 97.9 us -> none  [the longest x2 97.9 us: local(): lax.psum(edge_part(direction, own_table, flat_list, src_local, dst_index,...]
    gather x9 -> x0, local copies, waits for them, and re-layouts: 90.7 us -> none  [the longest x4 57.7 us: edge_part(): edge_diffs = weights[:, None] * (field_in[sources] - extended[targets])]
    all_to_all x7 -> x0, starting transfers between devices: 27.5 us -> none  [the longest x3 10.9 us: fetch(): lax.all_to_all(listed, 'vtx', split_axis=0, concat_axis=0, tiled=True)]
    all_to_all x7 -> x0, waiting for transfers between devices: 21.4 us -> none  [the longest x2 10.9 us: edge_part(): lax.all_to_all(outgoing, 'vtx', split_axis=0, concat_axis=0, tiled=True)]
    psum x1 -> x0, blocking collectives: 12.3 us -> none  [local(): right_side, degree = lax.psum((local_side, local_degree), 'edg')]
    add x2 -> x0, other arithmetic: 5.1 us -> none  [the longest x1 3.08 us: local(): solution = solution + direction]
  transfers between devices with their start and end apart: 10 -> 0, of which waited for: 6 -> 0; matrix products, arithmetic and copies ran while one was open for 19% -> 0% of each run, Pallas kernels for 0% -> 0%
where the time goes in v3:
time: 215 us; the launch traced here: 214 us
  Pallas kernels  202 us (94%)
  local copies, waits for them, and re-layouts  6.57 us (3%)
  other arithmetic  4.29 us (2%)
    pallas_call x3, Pallas kernels, run_stage(): pl.pallas_call(functools.partial(stage_kernel, stage, peers, groups, piec...  202 us

profile of v3, /device:TPU:0, one launch (start us, length us, event | category | flops | bytes accessed | tf_op | source)
XLA Modules:
  0.0 214.4 jit_solution(17216293704848899679)
XLA Ops:
  1.3 0.1 pad.7.clone
  1.4 0.1 pad.8.clone
  1.4 1.3 reshape_squeeze.3.refs_4_
  2.7 1.3 pad.4.refs_6_
  4.0 0.7 fusion.5
  4.8 0.7 sqrt_select_fusion
  5.5 0.8 fusion.1
  6.3 1.6 stack.51.refs_2_
  7.8 0.7 maximum_maximum_fusion.refs_3_
  8.6 72.2 %stage0.1 = (f32[2048,128]{1,0:T(8,128)}, f32[2048,128]{1,0:T(8,128)}, f32[16,128]{1,0:T(8,128)}, bf16[4096,256]{1,0:T(8,128)(2,1)}) custom-call(bf16[4096,128]{1,0:T(8,128)(2,1)} %refs_0_.1, s32[8,48]{1,0:T(8,128)} %bitcast.23, s32[8,4096]{1,0:T(8,128)} %stack.51.refs_2_, f32[8,4096]{1,0:T(8,128)} %maximum_maximum_fusion.refs_3_, ...), custom_call_target="tpu_custom_call" | custom-call | tf_op jit(solution)/shard_map/stage0/pallas_call | solution.py:424
  80.8 64.8 %stage1.1 = (f32[2048,128]{1,0:T(8,128)}, f32[2048,128]{1,0:T(8,128)}, f32[2048,128]{1,0:T(8,128)}, bf16[4096,256]{1,0:T(8,128)(2,1)}) custom-call(bf16[4096,256]{1,0:T(8,128)(2,1)} %get-tuple-element.12.refs_0_, s32[8,48]{1,0:T(8,128)} %bitcast.24, s32[8,4096]{1,0:T(8,128)} %stack.51.refs_2_, f32[8,4096]{1,0:T(8,128)} %maximum_maximum_fusion.refs_3_, ...), custom_call_target="tpu_custom_call" | custom-call | tf_op jit(solution)/shard_map/stage1/pallas_call | solution.py:424
  145.5 65.2 %stage2.1 = (f32[2048,128]{1,0:T(8,128)}, f32[32,128]{1,0:T(8,128)}) custom-call(bf16[4096,256]{1,0:T(8,128)(2,1)} %get-tuple-element.16.refs_0_, s32[8,48]{1,0:T(8,128)} %bitcast.25, s32[8,4096]{1,0:T(8,128)} %stack.51.refs_2_, f32[8,4096]{1,0:T(8,128)} %maximum_maximum_fusion.refs_3_, s32[1,384]{1,0:T(1,128)} %reshape_squeeze.3.refs_4_, ...), custom_call_target="tpu_custom_call" | custom-call | tf_op jit(solution)/shard_map/stage2/pallas_call | solution.py:424
  210.8 1.3 fusion.2
  212.1 2.3 %copy.11 = f32[2048,128]{1,0:T(8,128)} copy(f32[2048,128]{1,0:T(8,128)} %get-tuple-element.32) | data formatting | bytes 2097152
  (2 shorter events, 0.0 us)

commit v4 on v3

--- a/solution.py
+++ b/solution.py
@@ -42,9 +42,11 @@
 
 
 def signed(src, dst, shape, axis):
-    at = lax.broadcasted_iota(jnp.int32, shape, axis)
-    value = jnp.where(at == src, 1.0, jnp.where(at == dst, -1.0, 0.0))
-    return value.astype(jnp.bfloat16)
+    at = lax.broadcasted_iota(jnp.int16, shape, axis)
+    one, none = jnp.ones(shape, jnp.bfloat16), jnp.zeros(shape, jnp.bfloat16)
+    is_src = at == jnp.broadcast_to(src.astype(jnp.int16), shape)
+    is_dst = at == jnp.broadcast_to(dst.astype(jnp.int16), shape)
+    return jnp.where(is_src, one, jnp.where(is_dst, -one, none))
 
 
 def halves(x):

time: 215 us -> 200 us (0.930)
  Pallas kernels: 202 us -> 187 us
    pallas_call x3, Pallas kernels: 202 us -> 187 us  [run_stage(): pl.pallas_call(functools.partial(stage_kernel, stage, peers, groups, piec...]
where the time goes in v4:
time: 200 us; the launch traced here: 199 us
  Pallas kernels  187 us (94%)
  local copies, waits for them, and re-layouts  6.57 us (3%)
  other arithmetic  4.29 us (2%)
    pallas_call x3, Pallas kernels, run_stage(): pl.pallas_call(functools.partial(stage_kernel, stage, peers, groups, piec...  187 us

profile of v4, /device:TPU:0, one launch (start us, length us, event | category | flops | bytes accessed | tf_op | source)
XLA Modules:
  0.0 199.4 jit_solution(2013895475913658024)
XLA Ops:
  1.3 0.1 pad.7.clone
  1.4 0.1 pad.8.clone
  1.4 1.3 reshape_squeeze.3.refs_4_
  2.7 1.3 pad.4.refs_6_
  4.0 0.7 fusion.5
  4.8 0.7 sqrt_select_fusion
  5.5 0.8 fusion.1
  6.3 1.6 stack.51.refs_2_
  7.8 0.7 maximum_maximum_fusion.refs_3_
  8.6 68.0 %stage0.1 = (f32[2048,128]{1,0:T(8,128)}, f32[2048,128]{1,0:T(8,128)}, f32[16,128]{1,0:T(8,128)}, bf16[4096,256]{1,0:T(8,128)(2,1)}) custom-call(bf16[4096,128]{1,0:T(8,128)(2,1)} %refs_0_.1, s32[8,48]{1,0:T(8,128)} %bitcast.23, s32[8,4096]{1,0:T(8,128)} %stack.51.refs_2_, f32[8,4096]{1,0:T(8,128)} %maximum_maximum_fusion.refs_3_, ...), custom_call_target="tpu_custom_call" | custom-call | tf_op jit(solution)/shard_map/stage0/pallas_call | solution.py:426
  76.6 59.9 %stage1.1 = (f32[2048,128]{1,0:T(8,128)}, f32[2048,128]{1,0:T(8,128)}, f32[2048,128]{1,0:T(8,128)}, bf16[4096,256]{1,0:T(8,128)(2,1)}) custom-call(bf16[4096,256]{1,0:T(8,128)(2,1)} %get-tuple-element.12.refs_0_, s32[8,48]{1,0:T(8,128)} %bitcast.24, s32[8,4096]{1,0:T(8,128)} %stack.51.refs_2_, f32[8,4096]{1,0:T(8,128)} %maximum_maximum_fusion.refs_3_, ...), custom_call_target="tpu_custom_call" | custom-call | tf_op jit(solution)/shard_map/stage1/pallas_call | solution.py:426
  136.5 59.3 %stage2.1 = (f32[2048,128]{1,0:T(8,128)}, f32[32,128]{1,0:T(8,128)}) custom-call(bf16[4096,256]{1,0:T(8,128)(2,1)} %get-tuple-element.16.refs_0_, s32[8,48]{1,0:T(8,128)} %bitcast.25, s32[8,4096]{1,0:T(8,128)} %stack.51.refs_2_, f32[8,4096]{1,0:T(8,128)} %maximum_maximum_fusion.refs_3_, s32[1,384]{1,0:T(1,128)} %reshape_squeeze.3.refs_4_, ...), custom_call_target="tpu_custom_call" | custom-call | tf_op jit(solution)/shard_map/stage2/pallas_call | solution.py:426
  195.8 1.3 fusion.2
  197.1 2.3 %copy.11 = f32[2048,128]{1,0:T(8,128)} copy(f32[2048,128]{1,0:T(8,128)} %get-tuple-element.32) | data formatting | bytes 2097152
  (2 shorter events, 0.0 us)
